TPU v7x, 256 devices: a whole 4x4x8 slice. The times are simulated.
256 devices in a mesh: orient: 16 (over z, y_hi), trow: 4 (over y_lo, core), tcol: 4 (over x).
Axes of the slice: x: 4, y: 4 (y_hi: 2, y_lo: 2; y = y_hi * 2 + y_lo), z: 8, core: 2. Of those that a mesh axis runs over, the one named last changes fastest.
Arguments:
- micrograph: float32 [512, 512], P('trow', 'tcol'), may hold values from -6 to 6
- templates: float32 [16, 256, 256], P('orient'), may hold values from -600 to 600
- fine_templates: float32 [256, 256, 256], P('orient'), may hold values from -600 to 600
- peak_rows: int32 [256], P(('trow', 'tcol')), may hold values from 0 to 127
- peak_cols: int32 [256], P(('trow', 'tcol')), may hold values from 0 to 127
- peak_count: int32 [16], P(('trow', 'tcol')), may hold values from 1 to 16, 128 in all
Outputs:
- snr_map: float32 [512, 512], P('trow', 'tcol')
- refined: float32 [256], P(('trow', 'tcol'))
Inputs may be any that keep to these rules, and one draw needn't show every extreme that they name: The live slots of tile g are its first peak_count[g] slots; the counts of all tiles sum to 128.
All inputs are finite; a program needn't handle non-finite values. No bound on the sum of `peak_count` on one device may be relied on, other than what follows from the above.
Results may differ from a plain program's by a relative error of at most 0.00027.
Values sent between devices are 32-bit elements; how exact they have to be, the bound alone decides.
A program may use at most 64 MiB of HBM per device.

v0:
```python
import jax
import jax.numpy as jnp
from jax import lax
from jax.sharding import PartitionSpec as P


def padded(block, sides, width):
    for axis, dim in sides:
        count = lax.axis_size(axis)
        forward = [(i, i + 1) for i in range(count - 1)]
        backward = [(target, source) for source, target in forward]
        low = lax.ppermute(
            lax.slice_in_dim(block, block.shape[dim] - width, None, axis=dim), axis, forward
        )
        high = lax.ppermute(lax.slice_in_dim(block, 0, width, axis=dim), axis, backward)
        block = jnp.concatenate([low, block, high], axis=dim)
    return block


def side_by_side(arrays, axis, split_dim, concat_dim, along):
    both = jnp.concatenate(arrays, axis=along)
    result, at, done = (
        lax.all_to_all(both, axis, split_axis=split_dim, concat_axis=concat_dim, tiled=True),
        0,
        [],
    )
    for a in arrays:
        done.append(lax.slice_in_dim(result, at, at + a.shape[along], axis=along))
        at += a.shape[along]
    return tuple(done)


def joined_along(parts, dim):
    parts = jnp.moveaxis(parts, 0, dim)
    shape = parts.shape
    return parts.reshape(*shape[:dim], shape[dim] * shape[dim + 1], *shape[dim + 2 :])


def copy_for_each(array, axis):
    length = lax.axis_size(axis)
    return lax.all_to_all(
        jnp.broadcast_to(array[None], (length, *array.shape)), axis, 0, 0, tiled=True
    )


def gather_directly(array, axis, dim):
    return joined_along(copy_for_each(array, axis), dim)


def over_copies(array, axis):
    return copy_for_each(array, axis).max(axis=0)


def product(left_side, right_side):
    return jnp.dot(
        left_side, right_side, precision=lax.Precision.HIGHEST, preferred_element_type=jnp.float32
    )


def normalize(stack):
    centered = stack - jnp.mean(stack, axis=(1, 2), keepdims=True)
    spread = jnp.mean(centered * centered, axis=(1, 2), keepdims=True)
    return centered / jnp.sqrt(spread + 1e-06)


def tables(length):
    numbers = jnp.arange(length, dtype=jnp.int32)
    phase = numbers[:, None] * numbers[None, :] % length
    angle = phase.astype(jnp.float32) * (2.0 * jnp.pi / length)
    return (jnp.cos(angle), jnp.sin(angle))


def stacked(halves, length):
    real_part = halves[:, :length]
    imag_part = halves[:, length:]
    upper = jnp.concatenate([real_part, imag_part], axis=1)
    lower = jnp.concatenate([imag_part, -real_part], axis=1)
    return jnp.concatenate([upper, lower], axis=0)


def per_device(micrograph, templates, fine_templates, peak_rows, peak_cols, peak_count):
    tile_size = micrograph.shape[0]
    proj_size = templates.shape[1]
    half_width = proj_size // 2
    length = tile_size + proj_size
    window = padded(micrograph, (("trow", 0), ("tcol", 1)), half_width)
    cos_table, sine_table = tables(length)
    first_section = product(window, jnp.concatenate([cos_table, -sine_table], axis=1))
    left_table = jnp.concatenate([cos_table, sine_table], axis=1)
    image_spec = product(left_table, stacked(first_section, length))
    image_re = image_spec[:, :length]
    image_im = image_spec[:, length:]
    normed = normalize(templates)
    orient_local = templates.shape[0]
    column_table = jnp.concatenate([cos_table[:proj_size], -sine_table[:proj_size]], axis=1)
    orient_index = 0
    partial_value = product(normed[orient_index], column_table)
    results = [
        product(
            jnp.concatenate([cos_table[:, :proj_size], sine_table[:, :proj_size]], axis=1),
            stacked(partial_value, length),
        )
    ]
    template_spec = jnp.stack(results, axis=0)
    inverse_left = jnp.concatenate([cos_table[:tile_size], sine_table[:tile_size]], axis=1)
    inverse_right = jnp.concatenate([cos_table[:, :tile_size], -sine_table[:, :tile_size]], axis=0)
    scale = 1.0 / (length * length)
    best_map = jnp.full((tile_size, tile_size), -1e30, jnp.float32)
    orient_index = 0
    temp_re = template_spec[orient_index, :, :length]
    temp_im = template_spec[orient_index, :, length:]
    zeta_re = image_re * temp_re + image_im * temp_im
    zeta_im = image_im * temp_re - image_re * temp_im
    upper = jnp.concatenate([zeta_re, zeta_im], axis=1)
    lower = jnp.concatenate([-zeta_im, zeta_re], axis=1)
    middle = product(inverse_left, jnp.concatenate([upper, lower], axis=0))
    correl = product(middle, inverse_right) * scale / proj_size
    best_map = jnp.maximum(best_map, correl)
    squares = correl * correl
    orient_count = orient_local * lax.axis_size("orient")
    band_best, band_total, band_squares = side_by_side(
        (best_map[None], correl[None], squares[None]), "orient", 1, 0, 2
    )
    band_mean = jnp.sum(band_total, axis=0) / orient_count
    band_snr = (jnp.max(band_best, axis=0) - band_mean) / jnp.sqrt(
        jnp.sum(band_squares, axis=0) / orient_count + 1e-05
    )
    snr_map = gather_directly(band_snr, "orient", 0)
    fine_flat = normalize(fine_templates).reshape(fine_templates.shape[0], proj_size * proj_size)

    def extract(row_start, col_start):
        return lax.dynamic_slice(window, (row_start, col_start), (proj_size, proj_size))

    slot_total = peak_rows.shape[0]
    patches = jax.vmap(extract)(peak_rows, peak_cols).reshape(slot_total, proj_size * proj_size)
    scores = product(patches, fine_flat.T) / proj_size
    local_best = jnp.max(scores, axis=1)
    best_fine = over_copies(local_best, "orient")
    live_slots = jnp.arange(slot_total, dtype=jnp.int32) < peak_count[0]
    refined = jnp.where(live_slots, best_fine, 0.0)
    return (snr_map, refined)


def solution(mesh):
    placed = (
        P("trow", "tcol"),
        P("orient", None, None),
        P("orient", None, None),
        P(("trow", "tcol")),
        P(("trow", "tcol")),
        P(("trow", "tcol")),
    )
    return jax.shard_map(
        per_device,
        mesh=mesh,
        in_specs=placed,
        out_specs=(P("trow", "tcol"), P(("trow", "tcol"))),
        check_vma=False,
    )
```

profile of v0, /device:TPU:8, one launch (start us, length us, event | category | flops | bytes accessed | tf_op | source)
XLA Modules:
  0.0 261.2 jit_solution(12523238348327250860)
XLA Ops:
  0.6 1.9 collective-permute-start
  2.6 3.6 %collective-permute-start.1 = (f32[128,128]{1,0:T(8,128)}, f32[128,128]{1,0:T(8,128)S(1)}, u32[]{:S(2)}, u32[]{:S(2)}) collective-permute-start(f32[128,128]{1,0:T(8,128)} %param.6), channel_id=1, source_target_pairs={{4,0},{8,4},{12,8},{5,1},{9,5},{13,9},{6,2},{10,6},{14,10},{7,3},{... | collective-permute-start | bytes 196616 | tf_op jit(solution)/shard_map/ppermute | solution.py:15
  6.2 2.4 fusion.48
  8.6 2.3 fusion.59
  17.4 2.0 fusion.40
  20.4 2.5 reduce_sum.58
  22.9 2.9 %multiply_reduce_fusion = f32[16]{0:T(128)S(1)} fusion(f32[16,256,256]{2,1,0:T(8,128)} %param.8, f32[16]{0:T(128)S(1)} %broadcast_multiply_fusion), kind=kLoop, calls=%fused_computation.4 | loop fusion | flops 3145712 | bytes 4194432 | tf_op jit(solution)/shard_map/reduce_sum | solution.py:62
  26.4 2.6 %subtract_divide_fusion = f32[16,256,256]{2,1,0:T(8,128)} fusion(f32[16,256,256]{2,1,0:T(8,128)S(1)} %copy-done, f32[16]{0:T(128)S(1)} %add_sqrt_fusion, f32[16]{0:T(128)S(1)} %broadcast_multiply_fusion), kind=kLoop, calls=%fused_computation.5 | loop fusion | flops 2097152 | bytes 8388736 | tf_op jit(solution)/shard_map/div | solution.py:63
  29.1 2.1 fusion.22
  31.3 3.4 %collective-permute-start.2 = (f32[384,128]{1,0:T(8,128)S(1)}, f32[384,128]{1,0:T(8,128)S(1)}, u32[]{:S(2)}, u32[]{:S(2)}) collective-permute-start(f32[384,128]{1,0:T(8,128)S(1)} %constant_dynamic-update-slice_fusion), channel_id=1, source_target_pairs={{0,1},{1,2},{2,3},{4,5},{5,6},{6,7},{8,9},{9,10},{10,11},{12,13},{... | collective-permute-start | bytes 589832 | tf_op jit(solution)/shard_map/ppermute | solution.py:12
  34.7 1.5 collective-permute-start.3
  36.2 1.7 collective-permute-done.2
  37.9 4.4 %collective-permute-done.3 = f32[384,128]{1,0:T(8,128)S(1)} collective-permute-done((f32[384,128]{1,0:T(8,128)S(1)}, f32[384,128]{1,0:T(8,128)S(1)}, u32[]{:S(2)}, u32[]{:S(2)}) %collective-permute-start.3) | collective-permute-done | bytes 196640 | tf_op jit(solution)/shard_map/ppermute | solution.py:15
  42.3 2.1 fusion.25
  44.4 3.1 %fusion.2 = f32[384,768]{1,0:T(8,128)S(1)} fusion(f32[384,384]{1,0:T(8,128)S(1)} %get-tuple-element.27, f32[384,384]{1,0:T(8,128)S(1)} %get-tuple-element.26, f32[384,768]{1,0:T(8,128)S(1)} %fusion.25, f32[384,384]{1,0:T(8,128)S(1)} %get-tuple-element.33, f32[384,384]{1,0:T(8,128)S(1)} %get-tuple-element.32), kind=kOutput, calls=%fused_computation.6 | convolution fusion | flops 2719383552 | bytes 4718592 | tf_op jit(solution)/shard_map/dot_general | solution.py:55
  48.6 1.5 fusion.8
  50.9 148.4 %while.1 = (s32[]{:T(128)}, f32[384,384]{1,0:T(8,128)S(1)}, s32[16,2]{0,1:T(2,128)S(1)}, f32[16,256,256]{2,0,1:T(8,128)}, s32[]{:T(128)}, /*index=5*/s32[]{:T(128)}) while((s32[]{:T(128)}, f32[384,384]{1,0:T(8,128)S(1)}, s32[16,2]{0,1:T(2,128)S(1)}, f32[16,256,256]{2,0,1:T(8,128)}, s32[]{:T(128)}, /*index=5*/s32[]{:T(128)}) %tuple.32), condition=%wide.while_cond, body=%wide.while_body.sunk | while | flops 2 | bytes 1572981 | solution.py:132
  51.7 1.4 dynamic-slice_bitcast_fusion.2
  53.4 7.0 %dynamic-update-slice.9 = f32[16,256,256]{2,0,1:T(8,128)} dynamic-update-slice(f32[16,256,256]{2,0,1:T(8,128)} %get-tuple-element.74, f32[1,256,256]{2,0,1:T(1,128)S(1)} %copy.43, s32[]{:T(128)} %get-tuple-element.71, s32[]{:T(128)} %constant.38.clone.1..sunk, s32[]{:T(128)} %constant.38.clone.1..sunk) | dynamic-update-slice | bytes 524292 | tf_op jit(solution)/shard_map/vmap()/gather
  61.0 1.4 dynamic-slice_bitcast_fusion.2
  62.7 7.0 %dynamic-update-slice.9 = f32[16,256,256]{2,0,1:T(8,128)} dynamic-update-slice(f32[16,256,256]{2,0,1:T(8,128)} %get-tuple-element.74, f32[1,256,256]{2,0,1:T(1,128)S(1)} %copy.43, s32[]{:T(128)} %get-tuple-element.71, s32[]{:T(128)} %constant.38.clone.1..sunk, s32[]{:T(128)} %constant.38.clone.1..sunk) | dynamic-update-slice | bytes 524292 | tf_op jit(solution)/shard_map/vmap()/gather
  70.3 1.4 dynamic-slice_bitcast_fusion.2
  72.0 7.0 %dynamic-update-slice.9 = f32[16,256,256]{2,0,1:T(8,128)} dynamic-update-slice(f32[16,256,256]{2,0,1:T(8,128)} %get-tuple-element.74, f32[1,256,256]{2,0,1:T(1,128)S(1)} %copy.43, s32[]{:T(128)} %get-tuple-element.71, s32[]{:T(128)} %constant.38.clone.1..sunk, s32[]{:T(128)} %constant.38.clone.1..sunk) | dynamic-update-slice | bytes 524292 | tf_op jit(solution)/shard_map/vmap()/gather
  79.6 1.4 dynamic-slice_bitcast_fusion.2
  81.3 7.0 %dynamic-update-slice.9 = f32[16,256,256]{2,0,1:T(8,128)} dynamic-update-slice(f32[16,256,256]{2,0,1:T(8,128)} %get-tuple-element.74, f32[1,256,256]{2,0,1:T(1,128)S(1)} %copy.43, s32[]{:T(128)} %get-tuple-element.71, s32[]{:T(128)} %constant.38.clone.1..sunk, s32[]{:T(128)} %constant.38.clone.1..sunk) | dynamic-update-slice | bytes 524292 | tf_op jit(solution)/shard_map/vmap()/gather
  90.5 7.0 %dynamic-update-slice.9 = f32[16,256,256]{2,0,1:T(8,128)} dynamic-update-slice(f32[16,256,256]{2,0,1:T(8,128)} %get-tuple-element.74, f32[1,256,256]{2,0,1:T(1,128)S(1)} %copy.43, s32[]{:T(128)} %get-tuple-element.71, s32[]{:T(128)} %constant.38.clone.1..sunk, s32[]{:T(128)} %constant.38.clone.1..sunk) | dynamic-update-slice | bytes 524292 | tf_op jit(solution)/shard_map/vmap()/gather
  98.1 1.4 dynamic-slice_bitcast_fusion.2
  99.8 7.0 %dynamic-update-slice.9 = f32[16,256,256]{2,0,1:T(8,128)} dynamic-update-slice(f32[16,256,256]{2,0,1:T(8,128)} %get-tuple-element.74, f32[1,256,256]{2,0,1:T(1,128)S(1)} %copy.43, s32[]{:T(128)} %get-tuple-element.71, s32[]{:T(128)} %constant.38.clone.1..sunk, s32[]{:T(128)} %constant.38.clone.1..sunk) | dynamic-update-slice | bytes 524292 | tf_op jit(solution)/shard_map/vmap()/gather
  107.4 1.4 dynamic-slice_bitcast_fusion.2
  109.1 7.0 %dynamic-update-slice.9 = f32[16,256,256]{2,0,1:T(8,128)} dynamic-update-slice(f32[16,256,256]{2,0,1:T(8,128)} %get-tuple-element.74, f32[1,256,256]{2,0,1:T(1,128)S(1)} %copy.43, s32[]{:T(128)} %get-tuple-element.71, s32[]{:T(128)} %constant.38.clone.1..sunk, s32[]{:T(128)} %constant.38.clone.1..sunk) | dynamic-update-slice | bytes 524292 | tf_op jit(solution)/shard_map/vmap()/gather
  118.4 7.0 %dynamic-update-slice.9 = f32[16,256,256]{2,0,1:T(8,128)} dynamic-update-slice(f32[16,256,256]{2,0,1:T(8,128)} %get-tuple-element.74, f32[1,256,256]{2,0,1:T(1,128)S(1)} %copy.43, s32[]{:T(128)} %get-tuple-element.71, s32[]{:T(128)} %constant.38.clone.1..sunk, s32[]{:T(128)} %constant.38.clone.1..sunk) | dynamic-update-slice | bytes 524292 | tf_op jit(solution)/shard_map/vmap()/gather
  126.0 1.4 dynamic-slice_bitcast_fusion.2
  127.7 7.0 %dynamic-update-slice.9 = f32[16,256,256]{2,0,1:T(8,128)} dynamic-update-slice(f32[16,256,256]{2,0,1:T(8,128)} %get-tuple-element.74, f32[1,256,256]{2,0,1:T(1,128)S(1)} %copy.43, s32[]{:T(128)} %get-tuple-element.71, s32[]{:T(128)} %constant.38.clone.1..sunk, s32[]{:T(128)} %constant.38.clone.1..sunk) | dynamic-update-slice | bytes 524292 | tf_op jit(solution)/shard_map/vmap()/gather
  136.9 7.0 %dynamic-update-slice.9 = f32[16,256,256]{2,0,1:T(8,128)} dynamic-update-slice(f32[16,256,256]{2,0,1:T(8,128)} %get-tuple-element.74, f32[1,256,256]{2,0,1:T(1,128)S(1)} %copy.43, s32[]{:T(128)} %get-tuple-element.71, s32[]{:T(128)} %constant.38.clone.1..sunk, s32[]{:T(128)} %constant.38.clone.1..sunk) | dynamic-update-slice | bytes 524292 | tf_op jit(solution)/shard_map/vmap()/gather
  146.1 7.0 %dynamic-update-slice.9 = f32[16,256,256]{2,0,1:T(8,128)} dynamic-update-slice(f32[16,256,256]{2,0,1:T(8,128)} %get-tuple-element.74, f32[1,256,256]{2,0,1:T(1,128)S(1)} %copy.43, s32[]{:T(128)} %get-tuple-element.71, s32[]{:T(128)} %constant.38.clone.1..sunk, s32[]{:T(128)} %constant.38.clone.1..sunk) | dynamic-update-slice | bytes 524292 | tf_op jit(solution)/shard_map/vmap()/gather
  155.4 7.0 %dynamic-update-slice.9 = f32[16,256,256]{2,0,1:T(8,128)} dynamic-update-slice(f32[16,256,256]{2,0,1:T(8,128)} %get-tuple-element.74, f32[1,256,256]{2,0,1:T(1,128)S(1)} %copy.43, s32[]{:T(128)} %get-tuple-element.71, s32[]{:T(128)} %constant.38.clone.1..sunk, s32[]{:T(128)} %constant.38.clone.1..sunk) | dynamic-update-slice | bytes 524292 | tf_op jit(solution)/shard_map/vmap()/gather
  162.9 1.4 dynamic-slice_bitcast_fusion.2
  164.6 7.0 %dynamic-update-slice.9 = f32[16,256,256]{2,0,1:T(8,128)} dynamic-update-slice(f32[16,256,256]{2,0,1:T(8,128)} %get-tuple-element.74, f32[1,256,256]{2,0,1:T(1,128)S(1)} %copy.43, s32[]{:T(128)} %get-tuple-element.71, s32[]{:T(128)} %constant.38.clone.1..sunk, s32[]{:T(128)} %constant.38.clone.1..sunk) | dynamic-update-slice | bytes 524292 | tf_op jit(solution)/shard_map/vmap()/gather
  173.9 7.0 %dynamic-update-slice.9 = f32[16,256,256]{2,0,1:T(8,128)} dynamic-update-slice(f32[16,256,256]{2,0,1:T(8,128)} %get-tuple-element.74, f32[1,256,256]{2,0,1:T(1,128)S(1)} %copy.43, s32[]{:T(128)} %get-tuple-element.71, s32[]{:T(128)} %constant.38.clone.1..sunk, s32[]{:T(128)} %constant.38.clone.1..sunk) | dynamic-update-slice | bytes 524292 | tf_op jit(solution)/shard_map/vmap()/gather
  183.1 7.0 %dynamic-update-slice.9 = f32[16,256,256]{2,0,1:T(8,128)} dynamic-update-slice(f32[16,256,256]{2,0,1:T(8,128)} %get-tuple-element.74, f32[1,256,256]{2,0,1:T(1,128)S(1)} %copy.43, s32[]{:T(128)} %get-tuple-element.71, s32[]{:T(128)} %constant.38.clone.1..sunk, s32[]{:T(128)} %constant.38.clone.1..sunk) | dynamic-update-slice | bytes 524292 | tf_op jit(solution)/shard_map/vmap()/gather
  192.4 7.0 %dynamic-update-slice.9 = f32[16,256,256]{2,0,1:T(8,128)} dynamic-update-slice(f32[16,256,256]{2,0,1:T(8,128)} %get-tuple-element.74, f32[1,256,256]{2,0,1:T(1,128)S(1)} %copy.43, s32[]{:T(128)} %get-tuple-element.71, s32[]{:T(128)} %constant.38.clone.1..sunk, s32[]{:T(128)} %constant.38.clone.1..sunk) | dynamic-update-slice | bytes 524292 | tf_op jit(solution)/shard_map/vmap()/gather
  199.3 10.2 %fusion.34 = f32[16]{0:T(128)S(1)} fusion(f32[16,256,256]{2,0,1:T(8,128)} %get-tuple-element.9, f32[16,256,256]{2,1,0:T(8,128)} %subtract_divide_fusion), kind=kOutput, calls=%fused_computation.35 | convolution fusion | flops 201327088 | bytes 8388672 | tf_op jit(solution)/shard_map/dot_general | solution.py:55
  210.1 10.3 %all-to-all-start.2 = ((f32[16,1,16]{2,1,0:T(1,128)}), f32[16,1,16]{2,1,0:T(1,128)S(1)}, u32[]{:S(2)}, u32[]{:S(2)}) async-start(f32[16,1,16]{2,1,0:T(1,128)} %broadcast_in_dim.47), calls=%async_computation.2 | async-start | bytes 16384 | tf_op jit(solution)/shard_map/all_to_all | solution.py:41
  221.3 9.1 %all-to-all-done.2 = f32[16,1,16]{2,1,0:T(1,128)S(1)} async-done(((f32[16,1,16]{2,1,0:T(1,128)}), f32[16,1,16]{2,1,0:T(1,128)S(1)}, u32[]{:S(2)}, u32[]{:S(2)}) %all-to-all-start.2) | async-done | bytes 1056 | tf_op jit(solution)/shard_map/all_to_all | solution.py:41
  230.4 3.5 %all-to-all-start = ((f32[1,128,384]{2,0,1:T(1,128)}), f32[1,128,384]{2,0,1:T(1,128)S(1)}, u32[]{:S(2)}, u32[]{:S(2)}) async-start(f32[1,128,384]{2,0,1:T(1,128)} %copy.19), calls=%async_computation | async-start | bytes 393216 | tf_op jit(solution)/shard_map/all_to_all | solution.py:23
  234.6 11.2 %all-to-all-done = f32[1,128,384]{2,0,1:T(1,128)S(1)} async-done(((f32[1,128,384]{2,0,1:T(1,128)}), f32[1,128,384]{2,0,1:T(1,128)S(1)}, u32[]{:S(2)}, u32[]{:S(2)}) %all-to-all-start) | async-done | bytes 196640 | tf_op jit(solution)/shard_map/all_to_all | solution.py:23
  246.5 3.5 %all-to-all-start.1 = ((f32[16,8,128]{2,1,0:T(8,128)}), f32[16,8,128]{2,1,0:T(8,128)S(1)}, u32[]{:S(2)}, u32[]{:S(2)}) async-start(f32[16,8,128]{2,1,0:T(8,128)} %broadcast_in_dim.44), calls=%async_computation.1 | async-start | bytes 131072 | tf_op jit(solution)/shard_map/all_to_all | solution.py:41
  250.5 10.0 %all-to-all-done.1 = f32[16,8,128]{2,1,0:T(8,128)S(1)} async-done(((f32[16,8,128]{2,1,0:T(8,128)}), f32[16,8,128]{2,1,0:T(8,128)S(1)}, u32[]{:S(2)}, u32[]{:S(2)}) %all-to-all-start.1) | async-done | bytes 65568 | tf_op jit(solution)/shard_map/all_to_all | solution.py:41
  (112 shorter events, 37.1 us)
Async XLA Ops:
  0.6 30.6 %collective-permute-start = (f32[128,128]{1,0:T(8,128)}, f32[128,128]{1,0:T(8,128)S(1)}, u32[]{:S(2)}, u32[]{:S(2)}) collective-permute-start(f32[128,128]{1,0:T(8,128)} %param.6), channel_id=1, source_target_pairs={{0,4},{4,8},{8,12},{1,5},{5,9},{9,13},{2,6},{6,10},{10,14},{3,7},{... | collective-permute-start | bytes 196616 | tf_op jit(solution)/shard_map/ppermute | solution.py:12
  2.6 28.7 %collective-permute-start.1 = (f32[128,128]{1,0:T(8,128)}, f32[128,128]{1,0:T(8,128)S(1)}, u32[]{:S(2)}, u32[]{:S(2)}) collective-permute-start(f32[128,128]{1,0:T(8,128)} %param.6), channel_id=1, source_target_pairs={{4,0},{8,4},{12,8},{5,1},{9,5},{13,9},{6,2},{10,6},{14,10},{7,3},{... | collective-permute-start | bytes 196616 | tf_op jit(solution)/shard_map/ppermute | solution.py:15
  8.6 6.1 %copy-start.1 = (f32[1,256,256]{2,1,0:T(8,128)S(1)}, f32[1,256,256]{2,1,0:T(8,128)}, u32[]{:S(2)}) copy-start(f32[1,256,256]{2,1,0:T(8,128)} %param.7) | copy-start | bytes 786436
  22.9 3.4 %copy-start = (f32[16,256,256]{2,1,0:T(8,128)S(1)}, f32[16,256,256]{2,1,0:T(8,128)}, u32[]{:S(2)}) copy-start(f32[16,256,256]{2,1,0:T(8,128)} %param.8) | copy-start | bytes 12582916
  26.4 2.7 %copy-start.8 = (s32[16]{0:T(128)S(1)}, s32[16]{0:T(128)}, u32[]{:S(2)}) copy-start(s32[16]{0:T(128)} %param.9) | copy-start | bytes 196
  26.4 2.7 %copy-start.9 = (s32[16]{0:T(128)S(1)}, s32[16]{0:T(128)}, u32[]{:S(2)}) copy-start(s32[16]{0:T(128)} %param.10) | copy-start | bytes 196
  26.4 2.7 %copy-start.2 = (f32[384,256]{1,0:T(8,128)S(1)}, f32[384,256]{1,0:T(8,128)}, u32[]{:S(2)}) copy-start(f32[384,256]{1,0:T(8,128)} %slice.95) | copy-start | bytes 1179652
  26.4 2.7 %copy-start.3 = (f32[256,384]{1,0:T(8,128)S(1)}, f32[256,384]{1,0:T(8,128)}, u32[]{:S(2)}) copy-start(f32[256,384]{1,0:T(8,128)} %get-tuple-element.28) | copy-start | bytes 1179652
  26.4 2.7 %copy-start.4 = (f32[256,384]{1,0:T(8,128)S(1)}, f32[256,384]{1,0:T(8,128)}, u32[]{:S(2)}) copy-start(f32[256,384]{1,0:T(8,128)} %get-tuple-element.29) | copy-start | bytes 1179652
  29.0 2.2 copy-start.7
  31.3 6.6 %collective-permute-start.2 = (f32[384,128]{1,0:T(8,128)S(1)}, f32[384,128]{1,0:T(8,128)S(1)}, u32[]{:S(2)}, u32[]{:S(2)}) collective-permute-start(f32[384,128]{1,0:T(8,128)S(1)} %constant_dynamic-update-slice_fusion), channel_id=1, source_target_pairs={{0,1},{1,2},{2,3},{4,5},{5,6},{6,7},{8,9},{9,10},{10,11},{12,13},{... | collective-permute-start | bytes 589832 | tf_op jit(solution)/shard_map/ppermute | solution.py:12
  34.7 7.6 %collective-permute-start.3 = (f32[384,128]{1,0:T(8,128)S(1)}, f32[384,128]{1,0:T(8,128)S(1)}, u32[]{:S(2)}, u32[]{:S(2)}) collective-permute-start(f32[384,128]{1,0:T(8,128)S(1)} %constant_dynamic-update-slice_fusion), channel_id=1, source_target_pairs={{1,0},{2,1},{3,2},{5,4},{6,5},{7,6},{9,8},{10,9},{11,10},{13,12},{... | collective-permute-start | bytes 589832 | tf_op jit(solution)/shard_map/ppermute | solution.py:15
  47.6 0.9 copy-start.5
  47.6 1.0 copy-start.6
  210.1 20.3 %all-to-all-start.2 = ((f32[16,1,16]{2,1,0:T(1,128)}), f32[16,1,16]{2,1,0:T(1,128)S(1)}, u32[]{:S(2)}, u32[]{:S(2)}) async-start(f32[16,1,16]{2,1,0:T(1,128)} %broadcast_in_dim.47), calls=%async_computation.2 | async-start | bytes 16384 | tf_op jit(solution)/shard_map/all_to_all | solution.py:41
  230.4 15.4 %all-to-all-start = ((f32[1,128,384]{2,0,1:T(1,128)}), f32[1,128,384]{2,0,1:T(1,128)S(1)}, u32[]{:S(2)}, u32[]{:S(2)}) async-start(f32[1,128,384]{2,0,1:T(1,128)} %copy.19), calls=%async_computation | async-start | bytes 393216 | tf_op jit(solution)/shard_map/all_to_all | solution.py:23
  246.5 14.1 %all-to-all-start.1 = ((f32[16,8,128]{2,1,0:T(8,128)}), f32[16,8,128]{2,1,0:T(8,128)S(1)}, u32[]{:S(2)}, u32[]{:S(2)}) async-start(f32[16,8,128]{2,1,0:T(8,128)} %broadcast_in_dim.44), calls=%async_computation.1 | async-start | bytes 131072 | tf_op jit(solution)/shard_map/all_to_all | solution.py:41
where the time goes:
time: 264 us; the launch traced here: 261 us
  local copies, waits for them, and re-layouts  155 us (59%)
  waiting for transfers between devices  36.5 us (14%)
  starting transfers between devices  27.8 us (11%)
  matrix products  21.7 us (8%)
  other arithmetic  16.8 us (6%)
  between operations  2.95 us (1%)
    gather x80, local copies, waits for them, and re-layouts  148 us
    dot_general x7, matrix products, product(): jnp.dot(left_side, right_side, precision=lax.Precision.HIGHEST, preferred...  21.7 us
    all_to_all x2, waiting for transfers between devices, copy_for_each(): lax.all_to_all(jnp.broadcast_to(array[None], (length, *array.shape)), axi...  19.2 us
    all_to_all x2, starting transfers between devices, copy_for_each(): lax.all_to_all(jnp.broadcast_to(array[None], (length, *array.shape)), axi...  13.8 us
    all_to_all x1, waiting for transfers between devices, side_by_side(): lax.all_to_all(both, axis, split_axis=split_dim, concat_axis=concat_dim,...  11.2 us
    ppermute x2, starting transfers between devices, padded(): lax.ppermute(lax.slice_in_dim(block, block.shape[dim] - width, None, axis...  5.33 us
  transfers between devices with their start and end apart: 7, of which 5 were waited for; matrix products, arithmetic and copies ran while one was open for 9% of the time, Pallas kernels for 0%

commit v1 on v0

v1 whole, which is shorter than its diff:
```python
import jax
import jax.numpy as jnp
import numpy as np
from jax import lax
from jax.experimental import pallas as pl
from jax.experimental.pallas import tpu as pltpu
from jax.sharding import PartitionSpec as P

F32 = jnp.float32
BF16 = jnp.bfloat16
MESH = pl.DeviceIdType.MESH
T = 128
LEN = 3 * T
PROJ = 2 * T
GROUP = 16
SLOTS = 16
FINE = 16
HALF_ROOT3 = float(np.sqrt(3.0) / 2.0)
NEAR = [(dr, dc) for dr in (-1, 0, 1) for dc in (-1, 0, 1) if (dr, dc) != (0, 0)]
FAR_FIRST = (8, 7, 9, 6, 10, 5, 11, 4, 12, 3, 13, 1, 15, 2, 14)


def hi_lo(table):
    high = table.astype(BF16)
    low = (table - high.astype(np.float64)).astype(BF16)
    return np.stack([high, low])


def tables():
    b = np.arange(T)
    q = np.arange(T)
    k0 = 3 * q + 0.5
    k1 = 3 * np.arange(T // 2) + 1.5
    unit = 2.0 * np.pi / LEN
    a0 = unit * np.outer(b, k0)
    a1 = unit * np.outer(b, k1)
    row0 = np.block([[np.cos(a0), -np.sin(a0)], [np.sin(a0), np.cos(a0)]])
    row1 = np.concatenate([np.cos(a1), -np.sin(a1)], 1)
    col, inv = [], []
    for r in range(3):
        th = unit * np.outer(3 * q + r, b)
        col.append(np.concatenate([np.cos(th), np.sin(th)], 1))
        inv.append(np.concatenate([np.cos(th).T, -np.sin(th).T], 1))
    back = np.concatenate([np.cos(a0).T, -np.sin(a0).T, np.cos(a1).T, -np.sin(a1).T], 0)
    back = back * (2.0 / (LEN * LEN * PROJ))
    return (
        hi_lo(row0),
        hi_lo(row1),
        hi_lo(np.stack(col)),
        hi_lo(np.stack(inv)),
        hi_lo(back),
    )


def split(x):
    high = x.astype(BF16)
    return high, (x - high.astype(F32)).astype(BF16)


def dot(a, b):
    return jnp.dot(a, b, preferred_element_type=F32)


def table_times(high, low, x):
    xh, xl = split(x)
    return dot(high, xh) + dot(low, xh) + dot(high, xl)


def times_table(x, high, low):
    xh, xl = split(x)
    return dot(xh, high) + dot(xl, high) + dot(xh, low)


def rotated(z):
    last = z[:, 2 * T :]
    lane = lax.broadcasted_iota(jnp.int32, last.shape, 1)
    turned = pltpu.roll(last, T // 2, 1)
    turned = jnp.where(lane < T // 2, turned, -turned)
    return jnp.concatenate([z[:, T : 2 * T], -z[:, :T], turned], axis=1)


def with_rotated(z):
    return jnp.concatenate([z, rotated(z)], axis=0)


def kernel(
    tile, template, fine, rows, cols, row0, row1, col, inv, back,
    snr_out, best_out,
    win, tmpl, fine_v, row0_v, row1_v, col_v, inv_v, back_v, spec,
    scale, patch, acc, corr, bands, snr, finals,
    load_sem, halo_send, halo_recv, band_send, band_recv,
    snr_send, snr_recv, final_send, final_recv, near_sem, mid_sem, far_sem,
):
    o = lax.axis_index("orient")
    r = lax.axis_index("trow")
    c = lax.axis_index("tcol")

    loads = [
        pltpu.make_async_copy(src, dst, load_sem.at[i])
        for i, (src, dst) in enumerate(
            [
                (template.at[0], tmpl),
                (row0, row0_v),
                (row1, row1_v),
                (col, col_v),
                (tile, win.at[1, pl.ds(T, T)]),
                (fine, fine_v),
                (inv, inv_v),
                (back, back_v),
            ]
        )
    ]
    for load in loads:
        load.start()

    def other(step):
        return lax.rem(o + (step % GROUP), GROUP)

    def inside(dr, dc):
        checks = []
        if dr < 0:
            checks.append(r > 0)
        if dr > 0:
            checks.append(r < 3)
        if dc < 0:
            checks.append(c > 0)
        if dc > 0:
            checks.append(c < 3)
        out = checks[0]
        for check in checks[1:]:
            out = jnp.logical_and(out, check)
        return out

    mate = o + 1 - 2 * lax.rem(o, 2)
    barrier = pltpu.get_barrier_semaphore()
    for dr, dc in NEAR:
        @pl.when(inside(dr, dc))
        def _():
            pl.semaphore_signal(barrier, inc=1, device_id=(o, r + dr, c + dc), device_id_type=MESH)
    for peer in (other(2), other(14), mate):
        pl.semaphore_signal(barrier, inc=1, device_id=(peer, r, c), device_id_type=MESH)
    across = 3 - (r == 0).astype(jnp.int32) - (r == 3).astype(jnp.int32)
    along = 3 - (c == 0).astype(jnp.int32) - (c == 3).astype(jnp.int32)
    pl.semaphore_wait(barrier, across * along + 2)

    def halo(i):
        dr, dc = NEAR[i]
        return pltpu.make_async_remote_copy(
            src_ref=tile,
            dst_ref=win.at[1 - dc, pl.ds((1 - dr) * T, T)],
            send_sem=halo_send.at[i],
            recv_sem=halo_recv.at[i],
            device_id=(o, r + dr, c + dc),
            device_id_type=MESH,
        )

    for i, (dr, dc) in enumerate(NEAR):
        @pl.when(inside(dr, dc))
        def _():
            halo(i).start()

        @pl.when(jnp.logical_not(inside(dr, dc)))
        def _():
            win[1 + dc, pl.ds((1 + dr) * T, T)] = jnp.zeros((T, T), F32)

    for peer in (other(2), other(14)):
        pl.semaphore_signal(near_sem, inc=1, device_id=(peer, r, c), device_id_type=MESH)

    def row_dft(x0, x1, x2):
        if x2 is None:
            mixed = jnp.concatenate([x0 + 0.5 * x1, -HALF_ROOT3 * x1], axis=1)
            real = x0 - x1
        else:
            mixed = jnp.concatenate([x0 + 0.5 * (x1 - x2), -HALF_ROOT3 * (x1 + x2)], axis=1)
            real = x0 - x1 + x2
        return jnp.concatenate(
            [times_table(mixed, row0_v[0], row0_v[1]), times_table(real, row1_v[0], row1_v[1])], axis=1
        )

    def col_dft(b0, b1, b2):
        if b2 is None:
            total = b0 + b1
            even = b0 - 0.5 * b1
            odd = rotated(HALF_ROOT3 * b1)
        else:
            total = b0 + (b1 + b2)
            even = b0 - 0.5 * (b1 + b2)
            odd = rotated(HALF_ROOT3 * (b1 - b2))
        for k, z in enumerate((total, even + odd, even - odd)):
            yield table_times(col_v[0, k], col_v[1, k], with_rotated(z))

    for load in loads[:4]:
        load.wait()
    t = tmpl[...]
    t = t - jnp.sum(t, keepdims=True) * (1.0 / (PROJ * PROJ))
    spread = jnp.sum(t * t, keepdims=True) * (1.0 / (PROJ * PROJ))
    t = t / jnp.sqrt(spread + 1e-6)
    t = row_dft(t[:, :T], t[:, T:], None)
    for k, z in enumerate(col_dft(t[:T], t[T:], None)):
        spec[k] = z

    pl.semaphore_wait(near_sem, 2)
    for peer in (other(4), other(12)):
        pl.semaphore_signal(mid_sem, inc=1, device_id=(peer, r, c), device_id_type=MESH)

    loads[5].wait()

    @pl.loop(0, FINE)
    def _(f):
        t = fine_v[f]
        t = t - jnp.sum(t, keepdims=True) * (1.0 / (PROJ * PROJ))
        spread = jnp.sum(t * t, keepdims=True) * (1.0 / (PROJ * PROJ))
        fine_v[f] = t
        scale[pl.ds(f, 1)] = jnp.broadcast_to((1.0 / PROJ) / jnp.sqrt(spread + 1e-6), (1, T))

    pl.semaphore_wait(mid_sem, 2)
    pl.semaphore_signal(far_sem, inc=1, device_id=(other(8), r, c), device_id_type=MESH)

    loads[4].wait()
    loads[6].wait()
    loads[7].wait()
    for i, (dr, dc) in enumerate(NEAR):
        @pl.when(inside(-dr, -dc))
        def _():
            halo(i).wait_recv()

    w = row_dft(win[0], win[1], win[2])
    total = jnp.zeros((T, LEN), F32)
    lane = lax.broadcasted_iota(jnp.int32, (T, T), 1)
    for k, z in enumerate(col_dft(w[:T], w[T : 2 * T], w[2 * T :])):
        s = spec[k]
        last = s[:, 2 * T :]
        turned = pltpu.roll(last, T // 2, 1)
        re = jnp.concatenate([s[:, :T], s[:, :T], jnp.where(lane < T // 2, last, turned)], axis=1)
        im = jnp.concatenate(
            [s[:, T : 2 * T], s[:, T : 2 * T], jnp.where(lane < T // 2, turned, last)], axis=1
        )
        prod = z * re + rotated(z) * im
        total = total + table_times(inv_v[0, k], inv_v[1, k], with_rotated(prod))
    corr[...] = times_table(total, back_v[0], back_v[1]).reshape(GROUP, 8, T)

    pl.semaphore_wait(far_sem, 1)

    def band_copy(step, owner):
        return pltpu.make_async_remote_copy(
            src_ref=corr.at[other(step)],
            dst_ref=bands.at[owner],
            send_sem=band_send.at[step],
            recv_sem=band_recv.at[step],
            device_id=(other(step), r, c),
            device_id_type=MESH,
        )

    def spread_copy(buffer, sends, recvs, step, owner):
        return pltpu.make_async_remote_copy(
            src_ref=buffer.at[owner],
            dst_ref=buffer.at[owner],
            send_sem=sends.at[step],
            recv_sem=recvs.at[step],
            device_id=(other(step), r, c),
            device_id_type=MESH,
        )

    for step in FAR_FIRST:
        band_copy(step, o).start()
    bands[o] = corr[o]

    fine_lane = lax.broadcasted_iota(jnp.int32, (PROJ, T), 1)

    @pl.loop(0, SLOTS // 4)
    def _(block):
        for k in range(4):
            row = rows[block * 4 + k]
            column = cols[block * 4 + k]
            shift = lax.rem(T - column, T)
            parts = [pltpu.roll(win[j, pl.ds(row, PROJ)], shift, 1) for j in range(3)]
            for j in range(2):
                patch[k, j] = jnp.where(fine_lane < T - column, parts[j], parts[j + 1])

        @pl.loop(0, FINE // 4)
        def _(group):
            def step(i, sums):
                sums = list(sums)
                at = pl.ds(pl.multiple_of(i * 8, 8), 8)
                for j in range(2):
                    ps = [patch[k, j, at] for k in range(4)]
                    for m in range(4):
                        t = fine_v[group * 4 + m, at, pl.ds(j * T, T)]
                        for k in range(4):
                            sums[k * 4 + m] = sums[k * 4 + m] + ps[k] * t
                return tuple(sums)

            sums = lax.fori_loop(
                0, PROJ // 8, step, tuple(jnp.zeros((8, T), F32) for _ in range(16)), unroll=2
            )
            for k in range(4):
                for m in range(4):
                    acc[(block * 4 + k) * FINE + group * 4 + m] = sums[k * 4 + m]

    scores = jnp.sum(acc[...], axis=1).reshape(SLOTS, FINE, T) * scale[...][None]
    scores = jnp.sum(scores, axis=2, keepdims=True)
    local = jnp.broadcast_to(jnp.max(scores, axis=1), (SLOTS, T))
    at_row = lax.broadcasted_iota(jnp.int32, (SLOTS, T), 0)
    at_lane = lax.broadcasted_iota(jnp.int32, (SLOTS, T), 1)
    local = jnp.sum(jnp.where(at_row == at_lane, local, 0.0), axis=0, keepdims=True)
    finals[o] = jnp.broadcast_to(local, (8, T))
    for step in FAR_FIRST:
        spread_copy(finals, final_send, final_recv, step, o).start()

    for step in FAR_FIRST:
        band_copy(step, other(-step)).wait_recv()
    best = bands[0]
    added = bands[0]
    squares = bands[0] * bands[0]
    for k in range(1, GROUP):
        value = bands[k]
        best = jnp.maximum(best, value)
        added = added + value
        squares = squares + value * value
    snr[o] = (best - added / GROUP) / jnp.sqrt(squares / GROUP + 1e-5)
    for step in FAR_FIRST:
        spread_copy(snr, snr_send, snr_recv, step, o).start()

    for step in FAR_FIRST:
        spread_copy(finals, final_send, final_recv, step, other(-step)).wait_recv()
    best_fine = finals[0]
    for k in range(1, GROUP):
        best_fine = jnp.maximum(best_fine, finals[k])
    best_out[...] = best_fine

    for step in FAR_FIRST:
        spread_copy(snr, snr_send, snr_recv, step, other(-step)).wait_recv()
    snr_out[...] = snr[...].reshape(T, T)

    for i, (dr, dc) in enumerate(NEAR):
        @pl.when(inside(dr, dc))
        def _():
            halo(i).wait_send()
    for step in FAR_FIRST:
        band_copy(step, o).wait_send()
        spread_copy(finals, final_send, final_recv, step, o).wait_send()
        spread_copy(snr, snr_send, snr_recv, step, o).wait_send()


def per_device(micrograph, templates, fine_templates, peak_rows, peak_cols, peak_count):
    consts = [jnp.asarray(x) for x in tables()]
    any_spec = pl.BlockSpec(memory_space=pl.ANY)
    smem = pl.BlockSpec(memory_space=pltpu.SMEM)
    vmem = pl.BlockSpec(memory_space=pltpu.VMEM)
    dma = pltpu.SemaphoreType.DMA
    regular = pltpu.SemaphoreType.REGULAR
    snr, best = pl.pallas_call(
        kernel,
        out_shape=(
            jax.ShapeDtypeStruct((T, T), F32),
            jax.ShapeDtypeStruct((8, T), F32),
        ),
        in_specs=[any_spec] * 3 + [smem] * 2 + [any_spec] * 5,
        out_specs=(vmem, vmem),
        scratch_shapes=[
            pltpu.VMEM((3, LEN, T), F32),
            pltpu.VMEM((PROJ, PROJ), F32),
            pltpu.VMEM((FINE, PROJ, PROJ), F32),
            pltpu.VMEM((2, 2 * T, 2 * T), BF16),
            pltpu.VMEM((2, T, T), BF16),
            pltpu.VMEM((2, 3, T, 2 * T), BF16),
            pltpu.VMEM((2, 3, T, 2 * T), BF16),
            pltpu.VMEM((2, LEN, T), BF16),
            pltpu.VMEM((3, T, LEN), F32),
            pltpu.VMEM((FINE, T), F32),
            pltpu.VMEM((4, 2, PROJ, T), F32),
            pltpu.VMEM((SLOTS * FINE, 8, T), F32),
            pltpu.VMEM((GROUP, 8, T), F32),
            pltpu.VMEM((GROUP, 8, T), F32),
            pltpu.VMEM((GROUP, 8, T), F32),
            pltpu.VMEM((GROUP, 8, T), F32),
            dma((8,)),
            dma((8,)),
            dma((8,)),
            dma((16,)),
            dma((16,)),
            dma((16,)),
            dma((16,)),
            dma((16,)),
            dma((16,)),
            regular,
            regular,
            regular,
        ],
        compiler_params=pltpu.CompilerParams(
            collective_id=0, has_side_effects=True
        ),
    )(micrograph, templates, fine_templates, peak_rows, peak_cols, *consts)
    slots = jnp.arange(SLOTS, dtype=jnp.int32)
    refined = jnp.where(slots < peak_count[0], best[0, :SLOTS], 0.0)
    return snr, refined


def solution(mesh):
    placed = (
        P("trow", "tcol"),
        P("orient", None, None),
        P("orient", None, None),
        P(("trow", "tcol")),
        P(("trow", "tcol")),
        P(("trow", "tcol")),
    )
    return jax.shard_map(
        per_device,
        mesh=mesh,
        in_specs=placed,
        out_specs=(P("trow", "tcol"), P(("trow", "tcol"))),
        check_vma=False,
    )
```

time: 264 us -> 40.5 us (0.15)
  the two profiles are of different devices: /device:TPU:8 before, /device:TPU:1 now
where the time goes in v1:
time: 40.5 us; the launch traced here: 40.4 us
  Pallas kernels  36.4 us (90%)
  local copies, waits for them, and re-layouts  1.47 us (4%)
  between operations  1.29 us (3%)
  other arithmetic  1.19 us (3%)
    pallas_call x1, Pallas kernels, per_device(): pl.pallas_call(kernel, out_shape=(jax.ShapeDtypeStruct((T, T), F32), jax....  36.4 us
    unnamed x1, local copies, waits for them, and re-layouts  1.47 us
    select_n x1, other arithmetic, per_device(): refined = jnp.where(slots < peak_count[0], best[0, :SLOTS], 0.0)  1.19 us

profile of v1, /device:TPU:1, one launch (start us, length us, event | category | flops | bytes accessed | tf_op | source)
XLA Modules:
  0.0 40.4 jit_solution(11182744460432841713)
XLA Ops:
  0.6 36.4 %shard_map.122 = (f32[128,128]{1,0:T(8,128)}, f32[8,128]{1,0:T(8,128)}) custom-call(f32[128,128]{1,0:T(8,128)} %tile.1, f32[1,256,256]{2,1,0:T(8,128)} %template.1, f32[16,256,256]{2,1,0:T(8,128)} %fine.1, s32[16]{0:T(128)} %rows.1, s32[16]{0:T(128)} %cols.1, bf16[2,256,256]{2,1,0:T(8,128)(2,1)} %constant.12.clone.row0, ...), custom_call_target="tpu_custom_call" | custom-call | tf_op jit(solution)/shard_map/pallas_call | solution.py:352
  37.7 1.2 %compare_select_fusion = f32[16]{0:T(128)} fusion(f32[8,128]{1,0:T(8,128)} %get-tuple-element.5, s32[]{:T(128)} %bitcast.3), kind=kLoop, calls=%fused_computation | loop fusion | flops 32 | bytes 132 | tf_op jit(solution)/shard_map/jit(_where)/select_n | solution.py:395
  38.9 1.5 %copy.15 = f32[128,128]{1,0:T(8,128)} copy(f32[128,128]{1,0:T(8,128)} %get-tuple-element.8) | data formatting | bytes 131072

commit v2 on v1

--- a/solution.py
+++ b/solution.py
@@ -87,7 +87,7 @@
     tile, template, fine, rows, cols, row0, row1, col, inv, back,
     snr_out, best_out,
     win, tmpl, fine_v, row0_v, row1_v, col_v, inv_v, back_v, spec,
-    scale, patch, acc, corr, bands, snr, finals,
+    sums, squares_v, patches, planes, corr, bands, snr, finals,
     load_sem, halo_send, halo_recv, band_send, band_recv,
     snr_send, snr_recv, final_send, final_recv, near_sem, mid_sem, far_sem,
 ):
@@ -199,19 +199,35 @@
     for k, z in enumerate(col_dft(t[:T], t[T:], None)):
         spec[k] = z
 
+    loads[5].wait()
+
+    @pl.loop(0, FINE)
+    def _(f):
+        part = jnp.sum(fine_v[f].reshape(PROJ // 8, 8, PROJ), axis=0)
+        sums[f] = part[:, :T] + part[:, T:]
+
+    mean = jnp.sum(sums[...], axis=(1, 2), keepdims=True) * (1.0 / (PROJ * PROJ))
+    sums[...] = jnp.broadcast_to(mean, (FINE, 8, T))
+
     pl.semaphore_wait(near_sem, 2)
     for peer in (other(4), other(12)):
         pl.semaphore_signal(mid_sem, inc=1, device_id=(peer, r, c), device_id_type=MESH)
 
-    loads[5].wait()
-
-    @pl.loop(0, FINE)
-    def _(f):
-        t = fine_v[f]
-        t = t - jnp.sum(t, keepdims=True) * (1.0 / (PROJ * PROJ))
-        spread = jnp.sum(t * t, keepdims=True) * (1.0 / (PROJ * PROJ))
-        fine_v[f] = t
-        scale[pl.ds(f, 1)] = jnp.broadcast_to((1.0 / PROJ) / jnp.sqrt(spread + 1e-6), (1, T))
+    @pl.loop(0, FINE // 2)
+    def _(pair):
+        at = pl.ds(pl.multiple_of(pair * 16, 16), 16)
+        below = pl.ds(pl.multiple_of(pair * 16 + T, 16), 16)
+        mean = jnp.concatenate([sums[pair * 2], sums[pair * 2 + 1]], axis=0)
+        mean = jnp.concatenate([mean, mean], axis=1)
+        total = jnp.zeros((16, PROJ), F32)
+        for i in range(PROJ // 8):
+            group = pl.ds(i * 8, 8)
+            x = jnp.concatenate([fine_v[pair * 2, group], fine_v[pair * 2 + 1, group]], axis=0) - mean
+            total = total + x * x
+            high, low = split(x)
+            planes[at, pl.ds(i * PROJ, PROJ)] = high
+            planes[below, pl.ds(i * PROJ, PROJ)] = low
+        squares_v[at] = total[:, :T] + total[:, T:]
 
     pl.semaphore_wait(mid_sem, 2)
     pl.semaphore_signal(far_sem, inc=1, device_id=(other(8), r, c), device_id_type=MESH)
@@ -265,41 +281,43 @@
         band_copy(step, o).start()
     bands[o] = corr[o]
 
-    fine_lane = lax.broadcasted_iota(jnp.int32, (PROJ, T), 1)
-
-    @pl.loop(0, SLOTS // 4)
-    def _(block):
-        for k in range(4):
-            row = rows[block * 4 + k]
-            column = cols[block * 4 + k]
-            shift = lax.rem(T - column, T)
-            parts = [pltpu.roll(win[j, pl.ds(row, PROJ)], shift, 1) for j in range(3)]
-            for j in range(2):
-                patch[k, j] = jnp.where(fine_lane < T - column, parts[j], parts[j + 1])
-
-        @pl.loop(0, FINE // 4)
-        def _(group):
-            def step(i, sums):
-                sums = list(sums)
-                at = pl.ds(pl.multiple_of(i * 8, 8), 8)
-                for j in range(2):
-                    ps = [patch[k, j, at] for k in range(4)]
-                    for m in range(4):
-                        t = fine_v[group * 4 + m, at, pl.ds(j * T, T)]
-                        for k in range(4):
-                            sums[k * 4 + m] = sums[k * 4 + m] + ps[k] * t
-                return tuple(sums)
-
-            sums = lax.fori_loop(
-                0, PROJ // 8, step, tuple(jnp.zeros((8, T), F32) for _ in range(16)), unroll=2
-            )
-            for k in range(4):
-                for m in range(4):
-                    acc[(block * 4 + k) * FINE + group * 4 + m] = sums[k * 4 + m]
-
-    scores = jnp.sum(acc[...], axis=1).reshape(SLOTS, FINE, T) * scale[...][None]
-    scores = jnp.sum(scores, axis=2, keepdims=True)
-    local = jnp.broadcast_to(jnp.max(scores, axis=1), (SLOTS, T))
+    part_lane = lax.broadcasted_iota(jnp.int32, (8, T), 1)
+
+    @pl.loop(0, SLOTS // 2)
+    def _(pair):
+        at = pl.ds(pl.multiple_of(pair * 16, 16), 16)
+        below = pl.ds(pl.multiple_of(pair * 16 + T, 16), 16)
+        row = [rows[pair * 2 + k] for k in range(2)]
+        column = [cols[pair * 2 + k] for k in range(2)]
+        for i in range(PROJ // 8):
+            both = []
+            for k in range(2):
+                shift = lax.rem(T - column[k], T)
+                parts = [pltpu.roll(win[j, pl.ds(row[k] + i * 8, 8)], shift, 1) for j in range(3)]
+                keep = part_lane < T - column[k]
+                both.append(
+                    jnp.concatenate([jnp.where(keep, parts[j], parts[j + 1]) for j in range(2)], axis=1)
+                )
+            high, low = split(jnp.concatenate(both, axis=0))
+            patches[at, pl.ds(i * PROJ, PROJ)] = high
+            patches[below, pl.ds(i * PROJ, PROJ)] = low
+
+    scores = lax.dot_general(
+        patches[...], planes[...], (((1,), (1,)), ((), ())), preferred_element_type=F32
+    )
+    scores = (scores[:T, :T] + (scores[:T, T:] + scores[T:, :T])) + scores[T:, T:]
+    at_row = lax.broadcasted_iota(jnp.int32, (T, T), 0)
+    at_lane = lax.broadcasted_iota(jnp.int32, (T, T), 1)
+    scores = jnp.where(at_row % 8 == at_lane % 8, scores, 0.0)
+    scores = jnp.sum(scores.reshape(SLOTS, 8, T), axis=1)
+    spread = jnp.sum(squares_v[...].T, axis=0, keepdims=True)
+    for far in (4, 2, 1):
+        scores = scores + pltpu.roll(scores, T - far, 1)
+        spread = spread + pltpu.roll(spread, T - far, 1)
+    scores = scores * ((1.0 / PROJ) / jnp.sqrt(spread * (1.0 / (PROJ * PROJ)) + 1e-6))
+    lane = lax.broadcasted_iota(jnp.int32, (SLOTS, T), 1)
+    local = jnp.max(jnp.where(lane % 8 == 0, scores, -jnp.inf), axis=1, keepdims=True)
+    local = jnp.broadcast_to(local, (SLOTS, T))
     at_row = lax.broadcasted_iota(jnp.int32, (SLOTS, T), 0)
     at_lane = lax.broadcasted_iota(jnp.int32, (SLOTS, T), 1)
     local = jnp.sum(jnp.where(at_row == at_lane, local, 0.0), axis=0, keepdims=True)
@@ -367,9 +385,10 @@
             pltpu.VMEM((2, 3, T, 2 * T), BF16),
             pltpu.VMEM((2, LEN, T), BF16),
             pltpu.VMEM((3, T, LEN), F32),
-            pltpu.VMEM((FINE, T), F32),
-            pltpu.VMEM((4, 2, PROJ, T), F32),
-            pltpu.VMEM((SLOTS * FINE, 8, T), F32),
+            pltpu.VMEM((FINE, 8, T), F32),
+            pltpu.VMEM((FINE * 8, T), F32),
+            pltpu.VMEM((PROJ, PROJ * PROJ // 8), BF16),
+            pltpu.VMEM((PROJ, PROJ * PROJ // 8), BF16),
             pltpu.VMEM((GROUP, 8, T), F32),
             pltpu.VMEM((GROUP, 8, T), F32),
             pltpu.VMEM((GROUP, 8, T), F32),

time: 40.5 us -> 33.8 us (0.83)
  Pallas kernels: 36.4 us -> 29.7 us
    pallas_call x1, Pallas kernels: 36.4 us -> 29.7 us  [per_device(): pl.pallas_call(kernel, out_shape=(jax.ShapeDtypeStruct((T, T), F32), jax....]
where the time goes in v2:
time: 33.8 us; the launch traced here: 33.7 us
  Pallas kernels  29.7 us (88%)
  local copies, waits for them, and re-layouts  1.47 us (4%)
  between operations  1.29 us (4%)
  other arithmetic  1.19 us (4%)
    pallas_call x1, Pallas kernels, per_device(): pl.pallas_call(kernel, out_shape=(jax.ShapeDtypeStruct((T, T), F32), jax....  29.7 us
    unnamed x1, local copies, waits for them, and re-layouts  1.47 us
    select_n x1, other arithmetic, per_device(): refined = jnp.where(slots < peak_count[0], best[0, :SLOTS], 0.0)  1.19 us

profile of v2, /device:TPU:1, one launch (start us, length us, event | category | flops | bytes accessed | tf_op | source)
XLA Modules:
  0.0 33.7 jit_solution(6606851647500605034)
XLA Ops:
  0.6 29.7 %shard_map.122 = (f32[128,128]{1,0:T(8,128)}, f32[8,128]{1,0:T(8,128)}) custom-call(f32[128,128]{1,0:T(8,128)} %tile.1, f32[1,256,256]{2,1,0:T(8,128)} %template.1, f32[16,256,256]{2,1,0:T(8,128)} %fine.1, s32[16]{0:T(128)} %rows.1, s32[16]{0:T(128)} %cols.1, bf16[2,256,256]{2,1,0:T(8,128)(2,1)} %constant.12.clone.row0, ...), custom_call_target="tpu_custom_call" | custom-call | tf_op jit(solution)/shard_map/pallas_call | solution.py:370
  31.0 1.2 %compare_select_fusion = f32[16]{0:T(128)} fusion(f32[8,128]{1,0:T(8,128)} %get-tuple-element.5, s32[]{:T(128)} %bitcast.3), kind=kLoop, calls=%fused_computation | loop fusion | flops 32 | bytes 132 | tf_op jit(solution)/shard_map/jit(_where)/select_n | solution.py:414
  32.2 1.5 %copy.15 = f32[128,128]{1,0:T(8,128)} copy(f32[128,128]{1,0:T(8,128)} %get-tuple-element.8) | data formatting | bytes 131072

commit v3 on v2

--- a/solution.py
+++ b/solution.py
@@ -14,16 +14,29 @@
 PROJ = 2 * T
 GROUP = 16
 SLOTS = 16
+BANDS = 8
+BAND = T // BANDS
 FINE = 16
 HALF_ROOT3 = float(np.sqrt(3.0) / 2.0)
 NEAR = [(dr, dc) for dr in (-1, 0, 1) for dc in (-1, 0, 1) if (dr, dc) != (0, 0)]
+ALONG_Z = (4, 3, 5, 2, 6, 1, 7)
 FAR_FIRST = (8, 7, 9, 6, 10, 5, 11, 4, 12, 3, 13, 1, 15, 2, 14)
 
 
 def hi_lo(table):
     high = table.astype(BF16)
     low = (table - high.astype(np.float64)).astype(BF16)
-    return np.stack([high, low])
+    return high, low
+
+
+def left_terms(table):
+    high, low = hi_lo(table)
+    return np.concatenate([high, low, high], axis=-1)
+
+
+def right_terms(table):
+    high, low = hi_lo(table)
+    return np.concatenate([high, high, low], axis=0)
 
 
 def tables():
@@ -44,11 +57,11 @@
     back = np.concatenate([np.cos(a0).T, -np.sin(a0).T, np.cos(a1).T, -np.sin(a1).T], 0)
     back = back * (2.0 / (LEN * LEN * PROJ))
     return (
-        hi_lo(row0),
-        hi_lo(row1),
-        hi_lo(np.stack(col)),
-        hi_lo(np.stack(inv)),
-        hi_lo(back),
+        right_terms(row0),
+        right_terms(row1),
+        left_terms(np.stack(col)),
+        left_terms(np.stack(inv)),
+        right_terms(back),
     )
 
 
@@ -61,14 +74,14 @@
     return jnp.dot(a, b, preferred_element_type=F32)
 
 
-def table_times(high, low, x):
-    xh, xl = split(x)
-    return dot(high, xh) + dot(low, xh) + dot(high, xl)
-
-
-def times_table(x, high, low):
-    xh, xl = split(x)
-    return dot(xh, high) + dot(xl, high) + dot(xh, low)
+def table_times(table, x):
+    high, low = split(x)
+    return dot(table, jnp.concatenate([high, high, low], axis=0))
+
+
+def times_table(x, table):
+    high, low = split(x)
+    return dot(jnp.concatenate([high, low, high], axis=1), table)
 
 
 def rotated(z):
@@ -84,10 +97,10 @@
 
 
 def kernel(
-    tile, template, fine, rows, cols, row0, row1, col, inv, back,
+    tile, template, fine, rows_in, cols_in, row0, row1, col, inv, back,
     snr_out, best_out,
     win, tmpl, fine_v, row0_v, row1_v, col_v, inv_v, back_v, spec,
-    sums, squares_v, patches, planes, corr, bands, snr, finals,
+    sums, squares_v, patches, planes, corr, bands, snr, finals, rows, cols,
     load_sem, halo_send, halo_recv, band_send, band_recv,
     snr_send, snr_recv, final_send, final_recv, near_sem, mid_sem, far_sem,
 ):
@@ -107,6 +120,8 @@
                 (fine, fine_v),
                 (inv, inv_v),
                 (back, back_v),
+                (rows_in, rows),
+                (cols_in, cols),
             ]
         )
     ]
@@ -174,7 +189,7 @@
             mixed = jnp.concatenate([x0 + 0.5 * (x1 - x2), -HALF_ROOT3 * (x1 + x2)], axis=1)
             real = x0 - x1 + x2
         return jnp.concatenate(
-            [times_table(mixed, row0_v[0], row0_v[1]), times_table(real, row1_v[0], row1_v[1])], axis=1
+            [times_table(mixed, row0_v[...]), times_table(real, row1_v[...])], axis=1
         )
 
     def col_dft(b0, b1, b2):
@@ -187,7 +202,7 @@
             even = b0 - 0.5 * (b1 + b2)
             odd = rotated(HALF_ROOT3 * (b1 - b2))
         for k, z in enumerate((total, even + odd, even - odd)):
-            yield table_times(col_v[0, k], col_v[1, k], with_rotated(z))
+            yield table_times(col_v[k], with_rotated(z))
 
     for load in loads[:4]:
         load.wait()
@@ -252,14 +267,14 @@
             [s[:, T : 2 * T], s[:, T : 2 * T], jnp.where(lane < T // 2, turned, last)], axis=1
         )
         prod = z * re + rotated(z) * im
-        total = total + table_times(inv_v[0, k], inv_v[1, k], with_rotated(prod))
-    corr[...] = times_table(total, back_v[0], back_v[1]).reshape(GROUP, 8, T)
+        total = total + table_times(inv_v[k], with_rotated(prod))
+    corr[...] = times_table(total, back_v[...]).reshape(BANDS, BAND, T)
 
     pl.semaphore_wait(far_sem, 1)
 
     def band_copy(step, owner):
         return pltpu.make_async_remote_copy(
-            src_ref=corr.at[other(step)],
+            src_ref=corr.at[lax.div(other(step), 2)],
             dst_ref=bands.at[owner],
             send_sem=band_send.at[step],
             recv_sem=band_recv.at[step],
@@ -267,20 +282,33 @@
             device_id_type=MESH,
         )
 
-    def spread_copy(buffer, sends, recvs, step, owner):
+    def final_copy(step, owner):
         return pltpu.make_async_remote_copy(
-            src_ref=buffer.at[owner],
-            dst_ref=buffer.at[owner],
-            send_sem=sends.at[step],
-            recv_sem=recvs.at[step],
+            src_ref=finals.at[owner],
+            dst_ref=finals.at[owner],
+            send_sem=final_send.at[step],
+            recv_sem=final_recv.at[step],
             device_id=(other(step), r, c),
             device_id_type=MESH,
         )
 
+    def snr_copy(step, owner):
+        return pltpu.make_async_remote_copy(
+            src_ref=snr.at[owner],
+            dst_ref=snr.at[owner],
+            send_sem=snr_send.at[step],
+            recv_sem=snr_recv.at[step],
+            device_id=(other(2 * step), r, c),
+            device_id_type=MESH,
+        )
+
     for step in FAR_FIRST:
         band_copy(step, o).start()
-    bands[o] = corr[o]
-
+    layer = lax.div(o, 2)
+    bands[o] = corr[layer]
+
+    loads[8].wait()
+    loads[9].wait()
     part_lane = lax.broadcasted_iota(jnp.int32, (8, T), 1)
 
     @pl.loop(0, SLOTS // 2)
@@ -323,7 +351,7 @@
     local = jnp.sum(jnp.where(at_row == at_lane, local, 0.0), axis=0, keepdims=True)
     finals[o] = jnp.broadcast_to(local, (8, T))
     for step in FAR_FIRST:
-        spread_copy(finals, final_send, final_recv, step, o).start()
+        final_copy(step, o).start()
 
     for step in FAR_FIRST:
         band_copy(step, other(-step)).wait_recv()
@@ -335,19 +363,19 @@
         best = jnp.maximum(best, value)
         added = added + value
         squares = squares + value * value
-    snr[o] = (best - added / GROUP) / jnp.sqrt(squares / GROUP + 1e-5)
+    snr[layer] = (best - added / GROUP) / jnp.sqrt(squares / GROUP + 1e-5)
+    for step in ALONG_Z:
+        snr_copy(step, layer).start()
+
     for step in FAR_FIRST:
-        spread_copy(snr, snr_send, snr_recv, step, o).start()
-
-    for step in FAR_FIRST:
-        spread_copy(finals, final_send, final_recv, step, other(-step)).wait_recv()
+        final_copy(step, other(-step)).wait_recv()
     best_fine = finals[0]
     for k in range(1, GROUP):
         best_fine = jnp.maximum(best_fine, finals[k])
     best_out[...] = best_fine
 
-    for step in FAR_FIRST:
-        spread_copy(snr, snr_send, snr_recv, step, other(-step)).wait_recv()
+    for step in ALONG_Z:
+        snr_copy(step, lax.div(other(-2 * step), 2)).wait_recv()
     snr_out[...] = snr[...].reshape(T, T)
 
     for i, (dr, dc) in enumerate(NEAR):
@@ -356,14 +384,14 @@
             halo(i).wait_send()
     for step in FAR_FIRST:
         band_copy(step, o).wait_send()
-        spread_copy(finals, final_send, final_recv, step, o).wait_send()
-        spread_copy(snr, snr_send, snr_recv, step, o).wait_send()
+        final_copy(step, o).wait_send()
+    for step in ALONG_Z:
+        snr_copy(step, layer).wait_send()
 
 
 def per_device(micrograph, templates, fine_templates, peak_rows, peak_cols, peak_count):
     consts = [jnp.asarray(x) for x in tables()]
     any_spec = pl.BlockSpec(memory_space=pl.ANY)
-    smem = pl.BlockSpec(memory_space=pltpu.SMEM)
     vmem = pl.BlockSpec(memory_space=pltpu.VMEM)
     dma = pltpu.SemaphoreType.DMA
     regular = pltpu.SemaphoreType.REGULAR
@@ -373,27 +401,29 @@
             jax.ShapeDtypeStruct((T, T), F32),
             jax.ShapeDtypeStruct((8, T), F32),
         ),
-        in_specs=[any_spec] * 3 + [smem] * 2 + [any_spec] * 5,
+        in_specs=[any_spec] * 10,
         out_specs=(vmem, vmem),
         scratch_shapes=[
             pltpu.VMEM((3, LEN, T), F32),
             pltpu.VMEM((PROJ, PROJ), F32),
             pltpu.VMEM((FINE, PROJ, PROJ), F32),
-            pltpu.VMEM((2, 2 * T, 2 * T), BF16),
-            pltpu.VMEM((2, T, T), BF16),
-            pltpu.VMEM((2, 3, T, 2 * T), BF16),
-            pltpu.VMEM((2, 3, T, 2 * T), BF16),
-            pltpu.VMEM((2, LEN, T), BF16),
+            pltpu.VMEM((6 * T, 2 * T), BF16),
+            pltpu.VMEM((3 * T, T), BF16),
+            pltpu.VMEM((3, T, 6 * T), BF16),
+            pltpu.VMEM((3, T, 6 * T), BF16),
+            pltpu.VMEM((3 * LEN, T), BF16),
             pltpu.VMEM((3, T, LEN), F32),
             pltpu.VMEM((FINE, 8, T), F32),
             pltpu.VMEM((FINE * 8, T), F32),
             pltpu.VMEM((PROJ, PROJ * PROJ // 8), BF16),
             pltpu.VMEM((PROJ, PROJ * PROJ // 8), BF16),
+            pltpu.VMEM((BANDS, BAND, T), F32),
+            pltpu.VMEM((GROUP, BAND, T), F32),
+            pltpu.VMEM((BANDS, BAND, T), F32),
             pltpu.VMEM((GROUP, 8, T), F32),
-            pltpu.VMEM((GROUP, 8, T), F32),
-            pltpu.VMEM((GROUP, 8, T), F32),
-            pltpu.VMEM((GROUP, 8, T), F32),
-            dma((8,)),
+            pltpu.SMEM((SLOTS,), jnp.int32),
+            pltpu.SMEM((SLOTS,), jnp.int32),
+            dma((10,)),
             dma((8,)),
             dma((8,)),
             dma((16,)),

time: 33.8 us -> 31.8 us (0.941)
  Pallas kernels: 29.7 us -> 27.6 us
    pallas_call x1, Pallas kernels: 29.7 us -> 27.6 us  [per_device(): pl.pallas_call(kernel, out_shape=(jax.ShapeDtypeStruct((T, T), F32), jax....]
where the time goes in v3:
time: 31.8 us; the launch traced here: 31.6 us
  Pallas kernels  27.6 us (87%)
  local copies, waits for them, and re-layouts  1.47 us (5%)
  between operations  1.29 us (4%)
  other arithmetic  1.19 us (4%)
    pallas_call x1, Pallas kernels, per_device(): pl.pallas_call(kernel, out_shape=(jax.ShapeDtypeStruct((T, T), F32), jax....  27.6 us
    unnamed x1, local copies, waits for them, and re-layouts  1.47 us
    select_n x1, other arithmetic, per_device(): refined = jnp.where(slots < peak_count[0], best[0, :SLOTS], 0.0)  1.19 us

profile of v3, /device:TPU:1, one launch (start us, length us, event | category | flops | bytes accessed | tf_op | source)
XLA Modules:
  0.0 31.6 jit_solution(409652398093005978)
XLA Ops:
  0.6 27.6 %shard_map.122 = (f32[128,128]{1,0:T(8,128)}, f32[8,128]{1,0:T(8,128)}) custom-call(f32[128,128]{1,0:T(8,128)} %tile.1, f32[1,256,256]{2,1,0:T(8,128)} %template.1, f32[16,256,256]{2,1,0:T(8,128)} %fine.1, s32[16]{0:T(128)} %rows_in.1, s32[16]{0:T(128)} %cols_in.1, bf16[768,256]{1,0:T(8,128)(2,1)} %constant.12.clone.row0, ...), custom_call_target="tpu_custom_call" | custom-call | tf_op jit(solution)/shard_map/pallas_call | solution.py:398
  28.9 1.2 %compare_select_fusion = f32[16]{0:T(128)} fusion(f32[8,128]{1,0:T(8,128)} %get-tuple-element.5, s32[]{:T(128)} %bitcast.3), kind=kLoop, calls=%fused_computation | loop fusion | flops 32 | bytes 132 | tf_op jit(solution)/shard_map/jit(_where)/select_n | solution.py:444
  30.1 1.5 %copy.15 = f32[128,128]{1,0:T(8,128)} copy(f32[128,128]{1,0:T(8,128)} %get-tuple-element.8) | data formatting | bytes 131072

commit v4 on v3

--- a/solution.py
+++ b/solution.py
@@ -29,39 +29,36 @@
     return high, low
 
 
-def left_terms(table):
-    high, low = hi_lo(table)
-    return np.concatenate([high, low, high], axis=-1)
-
-
-def right_terms(table):
-    high, low = hi_lo(table)
-    return np.concatenate([high, high, low], axis=0)
+def side_by_side(table):
+    return np.concatenate(hi_lo(table), axis=-1)
+
+
+def stacked(table):
+    return np.concatenate(hi_lo(table), axis=-2)
 
 
 def tables():
     b = np.arange(T)
-    q = np.arange(T)
-    k0 = 3 * q + 0.5
+    k0 = 3 * b + 0.5
     k1 = 3 * np.arange(T // 2) + 1.5
     unit = 2.0 * np.pi / LEN
-    a0 = unit * np.outer(b, k0)
-    a1 = unit * np.outer(b, k1)
-    row0 = np.block([[np.cos(a0), -np.sin(a0)], [np.sin(a0), np.cos(a0)]])
-    row1 = np.concatenate([np.cos(a1), -np.sin(a1)], 1)
-    col, inv = [], []
+    a0 = unit * np.outer(k0, b)
+    a1 = unit * np.outer(k1, b)
+    first0 = np.block([[np.cos(a0), np.sin(a0)], [-np.sin(a0), np.cos(a0)]])
+    first1 = np.concatenate([np.cos(a1), -np.sin(a1)], 0)
+    second = []
     for r in range(3):
-        th = unit * np.outer(3 * q + r, b)
-        col.append(np.concatenate([np.cos(th), np.sin(th)], 1))
-        inv.append(np.concatenate([np.cos(th).T, -np.sin(th).T], 1))
-    back = np.concatenate([np.cos(a0).T, -np.sin(a0).T, np.cos(a1).T, -np.sin(a1).T], 0)
+        cos, sin = np.cos(unit * np.outer(b, 3 * b + r)), np.sin(unit * np.outer(b, 3 * b + r))
+        second.append(np.block([[cos, -sin], [sin, cos]]))
+    second = np.stack(second)
+    back = np.concatenate([np.cos(a0).T, np.cos(a1).T, -np.sin(a0).T, -np.sin(a1).T], 1)
     back = back * (2.0 / (LEN * LEN * PROJ))
     return (
-        right_terms(row0),
-        right_terms(row1),
-        left_terms(np.stack(col)),
-        left_terms(np.stack(inv)),
-        right_terms(back),
+        side_by_side(first0),
+        side_by_side(first1),
+        stacked(second),
+        stacked(np.swapaxes(second, 1, 2)),
+        side_by_side(back),
     )
 
 
@@ -76,30 +73,25 @@
 
 def table_times(table, x):
     high, low = split(x)
+    depth = x.shape[0]
+    table = jnp.concatenate([table, table[:, :depth]], axis=1)
     return dot(table, jnp.concatenate([high, high, low], axis=0))
 
 
-def times_table(x, table):
+def times_terms(x, table):
     high, low = split(x)
-    return dot(jnp.concatenate([high, low, high], axis=1), table)
-
-
-def rotated(z):
-    last = z[:, 2 * T :]
-    lane = lax.broadcasted_iota(jnp.int32, last.shape, 1)
-    turned = pltpu.roll(last, T // 2, 1)
-    turned = jnp.where(lane < T // 2, turned, -turned)
-    return jnp.concatenate([z[:, T : 2 * T], -z[:, :T], turned], axis=1)
-
-
-def with_rotated(z):
-    return jnp.concatenate([z, rotated(z)], axis=0)
+    depth = x.shape[1]
+    return [high, low, high], [table[:depth], table]
+
+
+def joined_dot(left, right):
+    return dot(jnp.concatenate(left, axis=1), jnp.concatenate(right, axis=0))
 
 
 def kernel(
-    tile, template, fine, rows_in, cols_in, row0, row1, col, inv, back,
+    tile, template, fine, rows_in, cols_in, first0, first1, second, inv, back,
     snr_out, best_out,
-    win, tmpl, fine_v, row0_v, row1_v, col_v, inv_v, back_v, spec,
+    win, tmpl, fine_v, first0_v, first1_v, second_v, inv_v, back_v, spec,
     sums, squares_v, patches, planes, corr, bands, snr, finals, rows, cols,
     load_sem, halo_send, halo_recv, band_send, band_recv,
     snr_send, snr_recv, final_send, final_recv, near_sem, mid_sem, far_sem,
@@ -113,9 +105,9 @@
         for i, (src, dst) in enumerate(
             [
                 (template.at[0], tmpl),
-                (row0, row0_v),
-                (row1, row1_v),
-                (col, col_v),
+                (first0, first0_v),
+                (first1, first1_v),
+                (second, second_v),
                 (tile, win.at[1, pl.ds(T, T)]),
                 (fine, fine_v),
                 (inv, inv_v),
@@ -181,28 +173,31 @@
     for peer in (other(2), other(14)):
         pl.semaphore_signal(near_sem, inc=1, device_id=(peer, r, c), device_id_type=MESH)
 
-    def row_dft(x0, x1, x2):
+    def first_pass(x0, x1, x2):
         if x2 is None:
-            mixed = jnp.concatenate([x0 + 0.5 * x1, -HALF_ROOT3 * x1], axis=1)
+            mixed = jnp.concatenate([x0 + 0.5 * x1, -HALF_ROOT3 * x1], axis=0)
             real = x0 - x1
         else:
-            mixed = jnp.concatenate([x0 + 0.5 * (x1 - x2), -HALF_ROOT3 * (x1 + x2)], axis=1)
+            mixed = jnp.concatenate([x0 + 0.5 * (x1 - x2), -HALF_ROOT3 * (x1 + x2)], axis=0)
             real = x0 - x1 + x2
-        return jnp.concatenate(
-            [times_table(mixed, row0_v[...]), times_table(real, row1_v[...])], axis=1
-        )
-
-    def col_dft(b0, b1, b2):
-        if b2 is None:
-            total = b0 + b1
-            even = b0 - 0.5 * b1
-            odd = rotated(HALF_ROOT3 * b1)
+        a = table_times(first0_v[...], mixed)
+        b = table_times(first1_v[...], real)
+        return (
+            jnp.concatenate([a[:T], b[: T // 2]], axis=0),
+            jnp.concatenate([a[T:], b[T // 2 :]], axis=0),
+        )
+
+    def second_pass(re, im):
+        r0, r1 = re[:, :T], re[:, T : 2 * T]
+        i0, i1 = im[:, :T], im[:, T : 2 * T]
+        if re.shape[1] == LEN:
+            r2, i2 = re[:, 2 * T :], im[:, 2 * T :]
+            ra, rb, ia, ib = r1 + r2, HALF_ROOT3 * (r1 - r2), i1 + i2, HALF_ROOT3 * (i1 - i2)
         else:
-            total = b0 + (b1 + b2)
-            even = b0 - 0.5 * (b1 + b2)
-            odd = rotated(HALF_ROOT3 * (b1 - b2))
-        for k, z in enumerate((total, even + odd, even - odd)):
-            yield table_times(col_v[k], with_rotated(z))
+            ra, rb, ia, ib = r1, HALF_ROOT3 * r1, i1, HALF_ROOT3 * i1
+        er, ei = r0 - 0.5 * ra, i0 - 0.5 * ia
+        for k, pair in enumerate(((r0 + ra, i0 + ia), (er + ib, ei - rb), (er - ib, ei + rb))):
+            yield joined_dot(*times_terms(jnp.concatenate(pair, axis=1), second_v[k]))
 
     for load in loads[:4]:
         load.wait()
@@ -210,8 +205,7 @@
     t = t - jnp.sum(t, keepdims=True) * (1.0 / (PROJ * PROJ))
     spread = jnp.sum(t * t, keepdims=True) * (1.0 / (PROJ * PROJ))
     t = t / jnp.sqrt(spread + 1e-6)
-    t = row_dft(t[:, :T], t[:, T:], None)
-    for k, z in enumerate(col_dft(t[:T], t[T:], None)):
+    for k, z in enumerate(second_pass(*first_pass(t[:T], t[T:], None))):
         spec[k] = z
 
     loads[5].wait()
@@ -255,20 +249,20 @@
         def _():
             halo(i).wait_recv()
 
-    w = row_dft(win[0], win[1], win[2])
-    total = jnp.zeros((T, LEN), F32)
-    lane = lax.broadcasted_iota(jnp.int32, (T, T), 1)
-    for k, z in enumerate(col_dft(w[:T], w[T : 2 * T], w[2 * T :])):
-        s = spec[k]
-        last = s[:, 2 * T :]
-        turned = pltpu.roll(last, T // 2, 1)
-        re = jnp.concatenate([s[:, :T], s[:, :T], jnp.where(lane < T // 2, last, turned)], axis=1)
-        im = jnp.concatenate(
-            [s[:, T : 2 * T], s[:, T : 2 * T], jnp.where(lane < T // 2, turned, last)], axis=1
-        )
-        prod = z * re + rotated(z) * im
-        total = total + table_times(inv_v[k], with_rotated(prod))
-    corr[...] = times_table(total, back_v[...]).reshape(BANDS, BAND, T)
+    w = [
+        jnp.concatenate([win[j, pl.ds(k * T, T)] for j in range(3)], axis=1) for k in range(3)
+    ]
+    left, right = [], []
+    for k, z in enumerate(second_pass(*first_pass(*w))):
+        wr, wi = z[:, :T], z[:, T:]
+        tr, ti = spec[k, :, :T], spec[k, :, T:]
+        prod = jnp.concatenate([wr * tr + wi * ti, wi * tr - wr * ti], axis=1)
+        terms = times_terms(prod, inv_v[k])
+        left += terms[0]
+        right += terms[1]
+    u = joined_dot(left, right)
+    u = jnp.concatenate([u[:, :T], u[:, T:]], axis=0)
+    corr[...] = table_times(back_v[...], u).reshape(BANDS, BAND, T)
 
     pl.semaphore_wait(far_sem, 1)
 
@@ -407,12 +401,12 @@
             pltpu.VMEM((3, LEN, T), F32),
             pltpu.VMEM((PROJ, PROJ), F32),
             pltpu.VMEM((FINE, PROJ, PROJ), F32),
-            pltpu.VMEM((6 * T, 2 * T), BF16),
-            pltpu.VMEM((3 * T, T), BF16),
-            pltpu.VMEM((3, T, 6 * T), BF16),
-            pltpu.VMEM((3, T, 6 * T), BF16),
-            pltpu.VMEM((3 * LEN, T), BF16),
-            pltpu.VMEM((3, T, LEN), F32),
+            pltpu.VMEM((2 * T, 4 * T), BF16),
+            pltpu.VMEM((T, 2 * T), BF16),
+            pltpu.VMEM((3, 4 * T, 2 * T), BF16),
+            pltpu.VMEM((3, 4 * T, 2 * T), BF16),
+            pltpu.VMEM((T, 2 * LEN), BF16),
+            pltpu.VMEM((3, LEN // 2, 2 * T), F32),
             pltpu.VMEM((FINE, 8, T), F32),
             pltpu.VMEM((FINE * 8, T), F32),
             pltpu.VMEM((PROJ, PROJ * PROJ // 8), BF16),

time: 31.8 us -> 31.6 us (level)
  no operation moved by 1% of the time
where the time goes in v4:
time: 31.6 us; the launch traced here: 31.4 us
  Pallas kernels  27.5 us (87%)
  local copies, waits for them, and re-layouts  1.47 us (5%)
  between operations  1.29 us (4%)
  other arithmetic  1.19 us (4%)
    pallas_call x1, Pallas kernels, per_device(): pl.pallas_call(kernel, out_shape=(jax.ShapeDtypeStruct((T, T), F32), jax....  27.5 us
    unnamed x1, local copies, waits for them, and re-layouts  1.47 us
    select_n x1, other arithmetic, per_device(): refined = jnp.where(slots < peak_count[0], best[0, :SLOTS], 0.0)  1.19 us

profile of v4, /device:TPU:1, one launch (start us, length us, event | category | flops | bytes accessed | tf_op | source)
XLA Modules:
  0.0 31.4 jit_solution(17419323211394093654)
XLA Ops:
  0.6 27.5 %shard_map.122 = (f32[128,128]{1,0:T(8,128)}, f32[8,128]{1,0:T(8,128)}) custom-call(f32[128,128]{1,0:T(8,128)} %tile.1, f32[1,256,256]{2,1,0:T(8,128)} %template.1, f32[16,256,256]{2,1,0:T(8,128)} %fine.1, s32[16]{0:T(128)} %rows_in.1, s32[16]{0:T(128)} %cols_in.1, bf16[256,512]{1,0:T(8,128)(2,1)} %constant.12.clone.first0, ...), custom_call_target="tpu_custom_call" | custom-call | tf_op jit(solution)/shard_map/pallas_call | solution.py:392
  28.8 1.2 %compare_select_fusion = f32[16]{0:T(128)} fusion(f32[8,128]{1,0:T(8,128)} %get-tuple-element.5, s32[]{:T(128)} %bitcast.3), kind=kLoop, calls=%fused_computation | loop fusion | flops 32 | bytes 132 | tf_op jit(solution)/shard_map/jit(_where)/select_n | solution.py:438
  29.9 1.5 %copy.15 = f32[128,128]{1,0:T(8,128)} copy(f32[128,128]{1,0:T(8,128)} %get-tuple-element.8) | data formatting | bytes 131072

commit v5 on v4

--- a/solution.py
+++ b/solution.py
@@ -89,12 +89,12 @@
 
 
 def kernel(
-    tile, template, fine, rows_in, cols_in, first0, first1, second, inv, back,
+    tile, template, fine, rows_in, cols_in, count_in, first0, first1, second, inv, back,
     snr_out, best_out,
     win, tmpl, fine_v, first0_v, first1_v, second_v, inv_v, back_v, spec,
-    sums, squares_v, patches, planes, corr, bands, snr, finals, rows, cols,
+    sums, squares_v, patches, planes, corr, bands, snr, finals, rows, cols, count,
     load_sem, halo_send, halo_recv, band_send, band_recv,
-    snr_send, snr_recv, final_send, final_recv, near_sem, mid_sem, far_sem,
+    snr_send, snr_recv, final_send, final_recv, near_sem, mate_sem,
 ):
     o = lax.axis_index("orient")
     r = lax.axis_index("trow")
@@ -114,6 +114,7 @@
                 (back, back_v),
                 (rows_in, rows),
                 (cols_in, cols),
+                (count_in, count),
             ]
         )
     ]
@@ -144,11 +145,11 @@
         @pl.when(inside(dr, dc))
         def _():
             pl.semaphore_signal(barrier, inc=1, device_id=(o, r + dr, c + dc), device_id_type=MESH)
-    for peer in (other(2), other(14), mate):
+    for peer in (other(2), other(14), other(4), other(12), mate):
         pl.semaphore_signal(barrier, inc=1, device_id=(peer, r, c), device_id_type=MESH)
     across = 3 - (r == 0).astype(jnp.int32) - (r == 3).astype(jnp.int32)
     along = 3 - (c == 0).astype(jnp.int32) - (c == 3).astype(jnp.int32)
-    pl.semaphore_wait(barrier, across * along + 2)
+    pl.semaphore_wait(barrier, across * along + 4)
 
     def halo(i):
         dr, dc = NEAR[i]
@@ -170,7 +171,7 @@
         def _():
             win[1 + dc, pl.ds((1 + dr) * T, T)] = jnp.zeros((T, T), F32)
 
-    for peer in (other(2), other(14)):
+    for peer in (other(4), other(12)):
         pl.semaphore_signal(near_sem, inc=1, device_id=(peer, r, c), device_id_type=MESH)
 
     def first_pass(x0, x1, x2):
@@ -219,8 +220,7 @@
     sums[...] = jnp.broadcast_to(mean, (FINE, 8, T))
 
     pl.semaphore_wait(near_sem, 2)
-    for peer in (other(4), other(12)):
-        pl.semaphore_signal(mid_sem, inc=1, device_id=(peer, r, c), device_id_type=MESH)
+    pl.semaphore_signal(mate_sem, inc=1, device_id=(mate, r, c), device_id_type=MESH)
 
     @pl.loop(0, FINE // 2)
     def _(pair):
@@ -238,8 +238,7 @@
             planes[below, pl.ds(i * PROJ, PROJ)] = low
         squares_v[at] = total[:, :T] + total[:, T:]
 
-    pl.semaphore_wait(mid_sem, 2)
-    pl.semaphore_signal(far_sem, inc=1, device_id=(other(8), r, c), device_id_type=MESH)
+    pl.semaphore_wait(mate_sem, 1)
 
     loads[4].wait()
     loads[6].wait()
@@ -263,8 +262,6 @@
     u = joined_dot(left, right)
     u = jnp.concatenate([u[:, :T], u[:, T:]], axis=0)
     corr[...] = table_times(back_v[...], u).reshape(BANDS, BAND, T)
-
-    pl.semaphore_wait(far_sem, 1)
 
     def band_copy(step, owner):
         return pltpu.make_async_remote_copy(
@@ -366,7 +363,9 @@
     best_fine = finals[0]
     for k in range(1, GROUP):
         best_fine = jnp.maximum(best_fine, finals[k])
-    best_out[...] = best_fine
+    loads[10].wait()
+    slot = lax.broadcasted_iota(jnp.int32, (8, T), 1)
+    best_out[...] = jnp.where(slot < count[0], best_fine, 0.0)
 
     for step in ALONG_Z:
         snr_copy(step, lax.div(other(-2 * step), 2)).wait_recv()
@@ -383,8 +382,18 @@
         snr_copy(step, layer).wait_send()
 
 
+def in_hbm(x):
+    return pltpu.with_memory_space_constraint(x, pltpu.HBM)
+
+
+def finish(snr, best, snr_out, refined):
+    snr_out[...] = snr[...]
+    refined[...] = best[0, :SLOTS]
+
+
 def per_device(micrograph, templates, fine_templates, peak_rows, peak_cols, peak_count):
-    consts = [jnp.asarray(x) for x in tables()]
+    consts = [in_hbm(jnp.asarray(x)) for x in tables()]
+    arrays = [in_hbm(x) for x in (micrograph, templates, fine_templates, peak_rows, peak_cols)]
     any_spec = pl.BlockSpec(memory_space=pl.ANY)
     vmem = pl.BlockSpec(memory_space=pltpu.VMEM)
     dma = pltpu.SemaphoreType.DMA
@@ -395,7 +404,7 @@
             jax.ShapeDtypeStruct((T, T), F32),
             jax.ShapeDtypeStruct((8, T), F32),
         ),
-        in_specs=[any_spec] * 10,
+        in_specs=[any_spec] * 11,
         out_specs=(vmem, vmem),
         scratch_shapes=[
             pltpu.VMEM((3, LEN, T), F32),
@@ -417,7 +426,8 @@
             pltpu.VMEM((GROUP, 8, T), F32),
             pltpu.SMEM((SLOTS,), jnp.int32),
             pltpu.SMEM((SLOTS,), jnp.int32),
-            dma((10,)),
+            pltpu.SMEM((1,), jnp.int32),
+            dma((11,)),
             dma((8,)),
             dma((8,)),
             dma((16,)),
@@ -426,17 +436,20 @@
             dma((16,)),
             dma((16,)),
             dma((16,)),
-            regular,
             regular,
             regular,
         ],
         compiler_params=pltpu.CompilerParams(
-            collective_id=0, has_side_effects=True
+            collective_id=0, has_side_effects=True, vmem_limit_bytes=48 * 1024 * 1024
         ),
-    )(micrograph, templates, fine_templates, peak_rows, peak_cols, *consts)
-    slots = jnp.arange(SLOTS, dtype=jnp.int32)
-    refined = jnp.where(slots < peak_count[0], best[0, :SLOTS], 0.0)
-    return snr, refined
+    )(*arrays, peak_count, *consts)
+    return pl.pallas_call(
+        finish,
+        out_shape=(jax.ShapeDtypeStruct((T, T), F32), jax.ShapeDtypeStruct((SLOTS,), F32)),
+        in_specs=[vmem, vmem],
+        out_specs=(vmem, vmem),
+        compiler_params=pltpu.CompilerParams(vmem_limit_bytes=1024 * 1024),
+    )(snr, best)
 
 
 def solution(mesh):

time: 31.6 us -> 29.5 us (0.934)
  local copies, waits for them, and re-layouts: 1.47 us -> 0 us
  other arithmetic: 1.19 us -> 0 us
  Pallas kernels: 27.5 us -> 28.1 us
    unnamed x1 -> x0, local copies, waits for them, and re-layouts: 1.47 us -> none
    select_n x1 -> x0, other arithmetic: 1.19 us -> none  [per_device(): refined = jnp.where(slots < peak_count[0], best[0, :SLOTS], 0.0)]
    pallas_call x0 -> x1, Pallas kernels: none -> 0.64 us  [per_device(): pl.pallas_call(finish, out_shape=(jax.ShapeDtypeStruct((T, T), F32), jax....]
where the time goes in v5:
time: 29.5 us; the launch traced here: 29.4 us
  Pallas kernels  28.1 us (95%)
  between operations  1.29 us (4%)
    pallas_call x1, Pallas kernels, per_device(): pl.pallas_call(kernel, out_shape=(jax.ShapeDtypeStruct((T, T), F32), jax....  27.5 us
    pallas_call x1, Pallas kernels, per_device(): pl.pallas_call(finish, out_shape=(jax.ShapeDtypeStruct((T, T), F32), jax....  0.64 us

profile of v5, /device:TPU:1, one launch (start us, length us, event | category | flops | bytes accessed | tf_op | source)
XLA Modules:
  0.0 29.4 jit_solution(10590520889403823001)
XLA Ops:
  1.3 27.5 %shard_map.122 = (f32[128,128]{1,0:T(8,128)S(1)}, f32[8,128]{1,0:T(8,128)S(1)}) custom-call(f32[128,128]{1,0:T(8,128)} %tile.1, f32[1,256,256]{2,1,0:T(8,128)} %template.1, f32[16,256,256]{2,1,0:T(8,128)} %fine.1, s32[16]{0:T(128)} %rows_in.1, s32[16]{0:T(128)} %cols_in.1, s32[1]{0:T(128)S(6)} %copy.13.count_in, bf16[256,512]{1,0:T(8,128)(2,1)} %constant.10.clone.first0, ...), custom_call_target="tpu_custom_call" | custom-call | tf_op jit(solution)/shard_map/pallas_call | solution.py:401
  28.7 0.6 %shard_map.123 = (f32[128,128]{1,0:T(8,128)}, f32[16]{0:T(128)}) custom-call(f32[128,128]{1,0:T(8,128)S(1)} %get-tuple-element.4.snr, f32[8,128]{1,0:T(8,128)S(1)} %get-tuple-element.5.best), custom_call_target="tpu_custom_call" | custom-call | tf_op jit(solution)/shard_map/pallas_call | solution.py:446

commit v6 on v5

--- a/solution.py
+++ b/solution.py
@@ -94,7 +94,7 @@
     win, tmpl, fine_v, first0_v, first1_v, second_v, inv_v, back_v, spec,
     sums, squares_v, patches, planes, corr, bands, snr, finals, rows, cols, count,
     load_sem, halo_send, halo_recv, band_send, band_recv,
-    snr_send, snr_recv, final_send, final_recv, near_sem, mate_sem,
+    snr_send, snr_recv, final_send, final_recv, near_sem, mid_sem, mate_sem,
 ):
     o = lax.axis_index("orient")
     r = lax.axis_index("trow")
@@ -118,8 +118,6 @@
             ]
         )
     ]
-    for load in loads:
-        load.start()
 
     def other(step):
         return lax.rem(o + (step % GROUP), GROUP)
@@ -145,11 +143,13 @@
         @pl.when(inside(dr, dc))
         def _():
             pl.semaphore_signal(barrier, inc=1, device_id=(o, r + dr, c + dc), device_id_type=MESH)
-    for peer in (other(2), other(14), other(4), other(12), mate):
+    for peer in (other(2), other(14), mate):
         pl.semaphore_signal(barrier, inc=1, device_id=(peer, r, c), device_id_type=MESH)
+    for load in loads:
+        load.start()
     across = 3 - (r == 0).astype(jnp.int32) - (r == 3).astype(jnp.int32)
     along = 3 - (c == 0).astype(jnp.int32) - (c == 3).astype(jnp.int32)
-    pl.semaphore_wait(barrier, across * along + 4)
+    pl.semaphore_wait(barrier, across * along + 2)
 
     def halo(i):
         dr, dc = NEAR[i]
@@ -171,7 +171,7 @@
         def _():
             win[1 + dc, pl.ds((1 + dr) * T, T)] = jnp.zeros((T, T), F32)
 
-    for peer in (other(4), other(12)):
+    for peer in (other(2), other(14)):
         pl.semaphore_signal(near_sem, inc=1, device_id=(peer, r, c), device_id_type=MESH)
 
     def first_pass(x0, x1, x2):
@@ -220,7 +220,8 @@
     sums[...] = jnp.broadcast_to(mean, (FINE, 8, T))
 
     pl.semaphore_wait(near_sem, 2)
-    pl.semaphore_signal(mate_sem, inc=1, device_id=(mate, r, c), device_id_type=MESH)
+    for peer in (other(4), other(12)):
+        pl.semaphore_signal(mid_sem, inc=1, device_id=(peer, r, c), device_id_type=MESH)
 
     @pl.loop(0, FINE // 2)
     def _(pair):
@@ -238,21 +239,30 @@
             planes[below, pl.ds(i * PROJ, PROJ)] = low
         squares_v[at] = total[:, :T] + total[:, T:]
 
-    pl.semaphore_wait(mate_sem, 1)
+    pl.semaphore_wait(mid_sem, 2)
+    pl.semaphore_signal(mate_sem, inc=1, device_id=(mate, r, c), device_id_type=MESH)
 
     loads[4].wait()
     loads[6].wait()
     loads[7].wait()
-    for i, (dr, dc) in enumerate(NEAR):
-        @pl.when(inside(-dr, -dc))
-        def _():
-            halo(i).wait_recv()
-
+    def arrived(columns):
+        for i, (dr, dc) in enumerate(NEAR):
+            if dc in columns:
+                @pl.when(inside(-dr, -dc))
+                def _():
+                    halo(i).wait_recv()
+
+    arrived((0,))
+    middle = first_pass(*[win[1, pl.ds(k * T, T)] for k in range(3)])
+    arrived((-1, 1))
+    sides = first_pass(
+        *[jnp.concatenate([win[j, pl.ds(k * T, T)] for j in (0, 2)], axis=1) for k in range(3)]
+    )
     w = [
-        jnp.concatenate([win[j, pl.ds(k * T, T)] for j in range(3)], axis=1) for k in range(3)
+        jnp.concatenate([side[:, :T], mid, side[:, T:]], axis=1) for side, mid in zip(sides, middle)
     ]
     left, right = [], []
-    for k, z in enumerate(second_pass(*first_pass(*w))):
+    for k, z in enumerate(second_pass(*w)):
         wr, wi = z[:, :T], z[:, T:]
         tr, ti = spec[k, :, :T], spec[k, :, T:]
         prod = jnp.concatenate([wr * tr + wi * ti, wi * tr - wr * ti], axis=1)
@@ -293,6 +303,7 @@
             device_id_type=MESH,
         )
 
+    pl.semaphore_wait(mate_sem, 1)
     for step in FAR_FIRST:
         band_copy(step, o).start()
     layer = lax.div(o, 2)
@@ -438,6 +449,7 @@
             dma((16,)),
             regular,
             regular,
+            regular,
         ],
         compiler_params=pltpu.CompilerParams(
             collective_id=0, has_side_effects=True, vmem_limit_bytes=48 * 1024 * 1024

time: 29.5 us -> 28.3 us (0.959)
  Pallas kernels: 28.1 us -> 26.9 us
    pallas_call x1, Pallas kernels: 27.5 us -> 26.2 us  [per_device(): pl.pallas_call(kernel, out_shape=(jax.ShapeDtypeStruct((T, T), F32), jax....]
where the time goes in v6:
time: 28.3 us; the launch traced here: 28.1 us
  Pallas kernels  26.9 us (95%)
  between operations  1.29 us (5%)
    pallas_call x1, Pallas kernels, per_device(): pl.pallas_call(kernel, out_shape=(jax.ShapeDtypeStruct((T, T), F32), jax....  26.2 us
    pallas_call x1, Pallas kernels, per_device(): pl.pallas_call(finish, out_shape=(jax.ShapeDtypeStruct((T, T), F32), jax....  0.64 us

profile of v6, /device:TPU:1, one launch (start us, length us, event | category | flops | bytes accessed | tf_op | source)
XLA Modules:
  0.0 28.1 jit_solution(1395247605516448000)
XLA Ops:
  1.3 26.2 %shard_map.122 = (f32[128,128]{1,0:T(8,128)S(1)}, f32[8,128]{1,0:T(8,128)S(1)}) custom-call(f32[128,128]{1,0:T(8,128)} %tile.1, f32[1,256,256]{2,1,0:T(8,128)} %template.1, f32[16,256,256]{2,1,0:T(8,128)} %fine.1, s32[16]{0:T(128)} %rows_in.1, s32[16]{0:T(128)} %cols_in.1, s32[1]{0:T(128)S(6)} %copy.13.count_in, bf16[256,512]{1,0:T(8,128)(2,1)} %constant.10.clone.first0, ...), custom_call_target="tpu_custom_call" | custom-call | tf_op jit(solution)/shard_map/pallas_call | solution.py:412
  27.5 0.6 %shard_map.123 = (f32[128,128]{1,0:T(8,128)}, f32[16]{0:T(128)}) custom-call(f32[128,128]{1,0:T(8,128)S(1)} %get-tuple-element.4.snr, f32[8,128]{1,0:T(8,128)S(1)} %get-tuple-element.5.best), custom_call_target="tpu_custom_call" | custom-call | tf_op jit(solution)/shard_map/pallas_call | solution.py:458
